TPU v7x, 1024 devices: a whole 8x8x8 slice. The times are simulated.
1024 devices in a mesh: gx: 16 (over z, core), gy: 16 (over y_lo, x), gz: 4 (over y_hi).
Axes of the slice: x: 8, y: 8 (y_hi: 4, y_lo: 2; y = y_hi * 2 + y_lo), z: 8, core: 2. Of those that a mesh axis runs over, the one named last changes fastest.
Arguments:
- links: bfloat16 [16, 16, 32, 2, 9, 64, 128], P('gx', 'gy', 'gz'), may hold values from -0.5 to 0.5
- null_vectors: bfloat16 [16, 16, 32, 2, 32, 128], P('gx', 'gy', 'gz'), may hold values from -1.796875 to 1.796875
- offsets: int32 [9, 4], replicated, may hold values from -1 to 1, as said below
- place: int32 [8, 8, 16, 1], replicated, may hold values from 0 to 31, as said below
Outputs:
- coarse_links: float32 [16, 4, 16, 9, 2048], P('gx', 'gz')
Inputs may be any that keep to these rules, and one draw needn't show every extreme that they name: The rows are the nine offsets zero, plus one and minus one along each of x, y, z, t, each once, in some order. `place`: for each cx and each aligned run of 4 values of cz, the values over all cy, those cz and all ct are each of 0 to 31 once.
All inputs are finite; a program needn't handle non-finite values.
Results may differ from a plain program's by a relative error of at most 0.0029.
Values may be sent and summed in bfloat16 or wider, within the bound.
No kernel may reach another device: no remote copies, remote signals or barrier semaphores. Data moves between devices by JAX's collectives and lax.ppermute only.
A program may use at most 32 MiB of HBM per device.

v0:
```python
import jax
import jax.numpy as jnp
from jax import lax
from jax.sharding import PartitionSpec as P

STANDARD = (
    (0, 0, 0, 0),
    (1, 0, 0, 0),
    (-1, 0, 0, 0),
    (0, 1, 0, 0),
    (0, -1, 0, 0),
    (0, 0, 1, 0),
    (0, 0, -1, 0),
    (0, 0, 0, 1),
    (0, 0, 0, -1),
)


def with_halo(block, sides, width):
    for axis, dim in sides:
        count = lax.axis_size(axis)
        forward = [(i, i + 1) for i in range(count - 1)]
        forward.append((count - 1, 0))
        backward = [(target, source) for source, target in forward]
        low = lax.ppermute(
            lax.slice_in_dim(block, block.shape[dim] - width, None, axis=dim), axis, forward
        )
        high = lax.ppermute(lax.slice_in_dim(block, 0, width, axis=dim), axis, backward)
        block = jnp.concatenate([low, block, high], axis=dim)
    return block


def partner(value, axis, distance):
    mask = 2**distance
    pairs = [(source, source ^ mask) for source in range(lax.axis_size(axis))]
    return lax.ppermute(value, axis, pairs)


def neighbour_blocks(neighbour):
    half_width = neighbour.shape[-1] // 2
    real_part = neighbour[..., :half_width]
    imag_part = neighbour[..., half_width:]
    upper_rows = jnp.concatenate([real_part, -imag_part], -1)
    lower_rows = jnp.concatenate([imag_part, real_part], -1)
    return jnp.concatenate([upper_rows, lower_rows], -2)


def conj_blocks(hopped):
    half_width = hopped.shape[-1] // 2
    hop_real = hopped[..., :half_width]
    hop_imag = hopped[..., half_width:]
    return jnp.concatenate([hopped, jnp.concatenate([hop_imag, -hop_real], -1)], -2)


def local(links, null_vectors, offsets, place):
    z_len = links.shape[2]
    t_len = links.shape[3]
    vec_count = null_vectors.shape[4]
    flat_width = 2 * vec_count * vec_count
    widened = with_halo(null_vectors, (("gx", 0), ("gy", 1), ("gz", 2)), 1)
    candidates = []
    for offset_row in STANDARD:
        shard_piece = widened[
            1 + offset_row[0], 1 + offset_row[1], 1 + offset_row[2] : 1 + offset_row[2] + z_len
        ]
        candidates.append(jnp.roll(shard_piece, -offset_row[3], axis=1))
    stacked = jnp.stack(candidates)
    standard_table = jnp.array(STANDARD, jnp.int32)
    matched = jnp.all(offsets[:, None, :] == standard_table[None, :, :], axis=-1).astype(jnp.int32)
    chosen = jnp.sum(matched * jnp.arange(9, dtype=jnp.int32)[None, :], axis=1)
    neighbour = jnp.take(stacked, chosen, axis=0)
    local_links = links[0, 0]
    hopped = jnp.einsum(
        "ztkrc,kztuc->ztkru",
        local_links,
        neighbour_blocks(neighbour),
        preferred_element_type=jnp.float32,
    ).astype(jnp.bfloat16)
    own_vectors = null_vectors[0, 0]
    coarse = jnp.einsum(
        "ztvq,ztkqu->ztkvu", own_vectors, conj_blocks(hopped), preferred_element_type=jnp.float32
    )
    x_sign = lax.axis_index("gx") % 2 * 2 - 1
    y_sign = lax.axis_index("gy") % 2 * 2 - 1
    z_sign = jnp.arange(z_len, dtype=jnp.int32) % 2 * 2 - 1
    t_sign = jnp.arange(t_len, dtype=jnp.int32) % 2 * 2 - 1
    outside = (
        (offsets[:, 0] == x_sign).astype(jnp.float32)[None, None, :]
        + (offsets[:, 1] == y_sign).astype(jnp.float32)[None, None, :]
        + (offsets[None, :, 2] == z_sign[:, None]).astype(jnp.float32)[:, None, :]
        + (offsets[None, :, 3] == t_sign[:, None]).astype(jnp.float32)[None, :, :]
    )
    is_self = jnp.all(offsets == 0, axis=1).astype(jnp.float32)
    spilled = jnp.sum((1.0 - outside)[..., None, None] * coarse, axis=2)
    contrib = (
        outside[..., None, None] * coarse + is_self[None, None, :, None, None] * spilled[:, :, None]
    )
    q_count = z_len // 2 * (t_len // 2)
    partial_value = contrib.reshape(z_len // 2, 2, t_len // 2, 2, 9, flat_width).sum(axis=(1, 3))
    partial_value = partial_value.reshape(q_count, 9, flat_width)
    partial_value = partial_value + partner(partial_value, "gx", 0)
    column_count = place.shape[1]
    my_column = lax.axis_index("gx") % 2
    line_places = lax.dynamic_slice(
        place,
        (lax.axis_index("gx") // 2, 0, lax.axis_index("gz") * (z_len // 2), 0),
        (1, column_count, z_len // 2, t_len // 2),
    )
    line_places = line_places.reshape(column_count, q_count)
    capacity = column_count * q_count // 2
    incoming = lax.all_gather(partial_value[None], "gy", axis=0, tiled=True)
    row_count = incoming.shape[0]
    sender = jnp.arange(row_count, dtype=jnp.int32)
    positions = jnp.take(line_places, sender // 2, axis=0)
    is_mine = positions // capacity == my_column
    slot_index = positions % capacity
    onehot = (
        (slot_index[..., None] == jnp.arange(capacity, dtype=jnp.int32)) & is_mine[..., None]
    ).astype(jnp.float32)
    gathered = jnp.einsum("nqs,nqkf->skf", onehot, incoming, precision=lax.Precision.HIGHEST)
    return gathered[None, None]


def solution(mesh):
    placed = (
        P("gx", "gy", "gz", None, None, None, None),
        P("gx", "gy", "gz", None, None, None),
        P(),
        P(),
    )
    return jax.shard_map(
        local,
        mesh=mesh,
        in_specs=placed,
        out_specs=P("gx", "gz", None, None, None),
        check_vma=False,
    )
```

profile of v0, /device:TPU:1, one launch (start us, length us, event | category | flops | bytes accessed | tf_op | source)
XLA Modules:
  0.0 203.9 jit_solution(18227633378825398839)
XLA Ops:
  6.5 0.0 copy-start
  6.5 0.0 all-gather.3.cloned.1.call-start
  6.5 4.4 %collective-permute-start.1 = (bf16[1,1,8,2,32,128]{5,4,3,2,1,0:T(8,128)(2,1)}, bf16[1,1,8,2,32,128]{5,4,3,2,1,0:T(8,128)(2,1)}, u32[]{:S(2)}, u32[]{:S(2)}) collective-permute-start(bf16[1,1,8,2,32,128]{5,4,3,2,1,0:T(8,128)(2,1)} %param.6), channel_id=1, source_target_pairs={{0,64},{64,128},{128,192},{192,256},{256,320},{320,384},{384,448},... | collective-permute-start | bytes 393224 | tf_op jit(solution)/shard_map/ppermute | solution.py:25
  10.9 9.7 %collective-permute-start = (bf16[1,1,8,2,32,128]{5,4,3,2,1,0:T(8,128)(2,1)}, bf16[1,1,8,2,32,128]{5,4,3,2,1,0:T(8,128)(2,1)}, u32[]{:S(2)}, u32[]{:S(2)}) collective-permute-start(bf16[1,1,8,2,32,128]{5,4,3,2,1,0:T(8,128)(2,1)} %param.6), channel_id=1, source_target_pairs={{64,0},{128,64},{192,128},{256,192},{320,256},{384,320},{448,384},... | collective-permute-start | bytes 393224 | tf_op jit(solution)/shard_map/ppermute | solution.py:28
  20.7 1.2 compare_reduce_fusion.1
  21.9 0.8 slice_bitcast_fusion.3
  22.6 0.8 copy.50
  23.4 0.8 compare_reduce_fusion
  24.2 0.1 select_reduce_fusion
  24.3 0.5 compare_and_fusion
  24.8 0.5 fusion.48
  25.4 0.9 bitcast_dynamic-update-slice_fusion.2
  26.3 0.9 fusion.52
  27.2 0.8 fusion.43
  27.9 0.1 compare_convert_fusion
  28.0 0.1 convert_add_fusion
  28.1 1.2 convert_element_type.51
  29.3 1.3 pad_clamp_fusion
  30.5 0.0 collective-permute-done.1
  30.5 0.9 constant_dynamic-update-slice_fusion.2
  31.4 0.9 constant_dynamic-update-slice_fusion.1
  32.4 0.0 collective-permute-done
  32.4 0.9 constant_dynamic-update-slice_fusion
  33.3 1.9 collective-permute-start.3
  35.2 5.5 %collective-permute-start.2 = (bf16[3,1,8,2,32,128]{5,4,3,2,1,0:T(8,128)(2,1)S(1)}, bf16[3,1,8,2,32,128]{5,4,3,2,1,0:T(8,128)(2,1)S(1)}, u32[]{:S(2)}, u32[]{:S(2)}) collective-permute-start(bf16[3,1,8,2,32,128]{5,4,3,2,1,0:T(8,128)(2,1)S(1)} %constant_dynamic-update-slice_fusion), channel_id=1, source_target_pairs={{4,0},{8,4},{12,8},{16,12},{20,16},{24,20},{28,24},{32,28},{36,32}... | collective-permute-start | bytes 1179656 | tf_op jit(solution)/shard_map/ppermute | solution.py:28
  40.7 0.9 bitcast_dynamic-update-slice_fusion.1
  41.6 0.9 bitcast_dynamic-update-slice_fusion
  42.6 2.5 %collective-permute-done.3 = bf16[3,1,8,2,32,128]{5,4,3,2,1,0:T(8,128)(2,1)S(1)} collective-permute-done((bf16[3,1,8,2,32,128]{5,4,3,2,1,0:T(8,128)(2,1)S(1)}, bf16[3,1,8,2,32,128]{5,4,3,2,1,0:T(8,128)(2,1)S(1)}, u32[]{:S(2)}, u32[]{:S(2)}) %collective-permute-start.3) | collective-permute-done | bytes 393248 | tf_op jit(solution)/shard_map/ppermute | solution.py:25
  45.0 0.9 collective-permute-done.2
  46.0 1.9 collective-permute-start.5
  47.9 5.5 %collective-permute-start.4 = (bf16[3,3,1,2,32,128]{5,4,3,2,1,0:T(8,128)(2,1)S(1)}, bf16[3,3,1,2,32,128]{5,4,3,2,1,0:T(8,128)(2,1)S(1)}, u32[]{:S(2)}, u32[]{:S(2)}) collective-permute-start(bf16[3,3,1,2,32,128]{5,4,3,2,1,0:T(8,128)(2,1)S(1)} %get-tuple-element.11), channel_id=1, source_target_pairs={{1,0},{2,1},{3,2},{0,3},{5,4},{6,5},{7,6},{4,7},{9,8},{10,9},{11,1... | collective-permute-start | bytes 442376 | tf_op jit(solution)/shard_map/ppermute | solution.py:28
  53.5 2.0 collective-permute-done.4
  55.5 0.0 collective-permute-done.5
  55.6 0.0 copy-start.1
  55.6 1.0 copy-done.1
  56.6 2.2 %gather_fusion.1 = bf16[9,8,2,32,128]{4,3,2,1,0:T(8,128)(2,1)S(1)} fusion(bf16[9,8,2,32,128]{4,3,2,1,0:T(8,128)(2,1)} %copy-done.1, s32[1024]{0:T(1024)} %get-tuple-element.20), kind=kCustom, calls=%fused_computation.1 | custom fusion | bytes 2359332 | tf_op jit(solution)/shard_map/jit(_take)/gather | solution.py:71
  58.8 0.8 copy_select_fusion
  59.6 0.5 slice_negate_fusion.1
  60.1 0.0 copy-done
  60.1 1.8 convert_bitcast_fusion
  61.9 0.0 copy-start.2
  61.9 0.2 fusion.51
  62.2 0.7 copy-done.2
  62.8 0.0 copy-start.3
  62.8 2.6 %multiply_reduce_fusion = (f32[8,2,64,32]{2,3,1,0:T(8,128)S(1)}, f32[8,2,9,64,32]{3,4,2,1,0:T(8,128)S(1)}) fusion(f32[8,2,9]{2,1,0:T(2,128)S(1)} %get-tuple-element.15, bf16[1,1,8,2,32,128]{5,4,3,2,1,0:T(8,128)(2,1)S(1)} %copy-done.2, bf16[8,2,9,64,32]{3,4,2,1,0:T(8,128)(2,1)S(1)} %get-tuple-element.6, bf16[8,2,9,64,32]{3,4,2,1,0:T(8,128)(2,1)S(1)} %get-tuple-element.5, ...), kind=kOutput, calls=%fused_computation.22 | convolution fusion | flops 83132416 | bytes 3801664 | tf_op jit(solution)/shard_map/ztvq,ztkqu->ztkvu/dot_general | solution.py:80
  65.4 0.0 copy-done.3
  65.4 0.5 fusion.19
  65.9 1.4 reshape.286
  67.3 1.3 reduce_sum.44
  68.6 0.2 copy.62
  68.8 11.5 %collective-permute-start.6 = (f32[4,9,2048]{2,0,1:T(4,128)S(1)}, f32[4,9,2048]{2,0,1:T(4,128)S(1)}, u32[]{:S(2)}, u32[]{:S(2)}) collective-permute-start(f32[4,9,2048]{2,0,1:T(4,128)S(1)} %copy.62), channel_id=1, source_target_pairs={{0,64},{64,0},{128,192},{192,128},{256,320},{320,256},{384,448},{4... | collective-permute-start | bytes 884744 | tf_op jit(solution)/shard_map/ppermute | solution.py:36
  80.3 1.2 collective-permute-done.6
  81.5 0.2 copy_add_fusion
  81.8 1.0 copy.53
  82.7 0.0 all-gather.3.cloned.1.call-update
  82.8 0.8 constant_dynamic-slice_fusion
  83.5 0.7 gather_fusion
  84.2 0.1 copy.49
  84.4 103.5 %all-gather.3.cloned.1.call-done = f32[64,9,2048]{2,1,0:T(8,128)} async-done(((f32[4,9,2048]{2,1,0:T(8,128)}), f32[64,9,2048]{2,1,0:T(8,128)}) %all-gather.3.cloned.1.call-update) | async-done | bytes 4718608 | tf_op jit(solution)/shard_map/all_gather | solution.py:111
  187.8 9.2 %fusion.2 = f32[1,1,16,9,2048]{4,2,3,1,0:T(8,128)} fusion(f32[16,4,9,2048]{3,2,1,0:T(8,128)} %bitcast.73, s32[16,4]{0,1:T(4,128)S(1)} %add_select_fusion.1, pred[16,4]{0,1:T(4,128)(4,1)S(1)} %fusion.39), kind=kOutput, calls=%fused_computation.4 | convolution fusion | flops 226494464 | bytes 5898560 | tf_op jit(solution)/shard_map/nqs,nqkf->skf/dot_general | solution.py:120
  (14 shorter events, 0.2 us)
Async XLA Ops:
  6.5 53.6 %copy-start = (bf16[1,1,8,2,9,64,128]{6,5,4,3,2,1,0:T(8,128)(2,1)S(1)}, bf16[1,1,8,2,9,64,128]{6,5,4,3,2,1,0:T(8,128)(2,1)}, u32[]{:S(2)}) copy-start(bf16[1,1,8,2,9,64,128]{6,5,4,3,2,1,0:T(8,128)(2,1)} %param.5) | copy-start | bytes 7077892
  6.5 181.3 %all-gather.3.cloned.1.call-start = ((), (), s32[]{:S(2)}) async-start(), calls=%async_computation | async-start | bytes 8912896 | tf_op jit(solution)/shard_map/all_gather | solution.py:111
  6.5 24.0 %collective-permute-start.1 = (bf16[1,1,8,2,32,128]{5,4,3,2,1,0:T(8,128)(2,1)}, bf16[1,1,8,2,32,128]{5,4,3,2,1,0:T(8,128)(2,1)}, u32[]{:S(2)}, u32[]{:S(2)}) collective-permute-start(bf16[1,1,8,2,32,128]{5,4,3,2,1,0:T(8,128)(2,1)} %param.6), channel_id=1, source_target_pairs={{0,64},{64,128},{128,192},{192,256},{256,320},{320,384},{384,448},... | collective-permute-start | bytes 393224 | tf_op jit(solution)/shard_map/ppermute | solution.py:25
  10.9 21.5 %collective-permute-start = (bf16[1,1,8,2,32,128]{5,4,3,2,1,0:T(8,128)(2,1)}, bf16[1,1,8,2,32,128]{5,4,3,2,1,0:T(8,128)(2,1)}, u32[]{:S(2)}, u32[]{:S(2)}) collective-permute-start(bf16[1,1,8,2,32,128]{5,4,3,2,1,0:T(8,128)(2,1)} %param.6), channel_id=1, source_target_pairs={{64,0},{128,64},{192,128},{256,192},{320,256},{384,320},{448,384},... | collective-permute-start | bytes 393224 | tf_op jit(solution)/shard_map/ppermute | solution.py:28
  33.3 11.7 %collective-permute-start.3 = (bf16[3,1,8,2,32,128]{5,4,3,2,1,0:T(8,128)(2,1)S(1)}, bf16[3,1,8,2,32,128]{5,4,3,2,1,0:T(8,128)(2,1)S(1)}, u32[]{:S(2)}, u32[]{:S(2)}) collective-permute-start(bf16[3,1,8,2,32,128]{5,4,3,2,1,0:T(8,128)(2,1)S(1)} %constant_dynamic-update-slice_fusion), channel_id=1, source_target_pairs={{0,4},{4,8},{8,12},{12,16},{16,20},{20,24},{24,28},{28,32},{32,36}... | collective-permute-start | bytes 1179656 | tf_op jit(solution)/shard_map/ppermute | solution.py:25
  35.2 10.7 %collective-permute-start.2 = (bf16[3,1,8,2,32,128]{5,4,3,2,1,0:T(8,128)(2,1)S(1)}, bf16[3,1,8,2,32,128]{5,4,3,2,1,0:T(8,128)(2,1)S(1)}, u32[]{:S(2)}, u32[]{:S(2)}) collective-permute-start(bf16[3,1,8,2,32,128]{5,4,3,2,1,0:T(8,128)(2,1)S(1)} %constant_dynamic-update-slice_fusion), channel_id=1, source_target_pairs={{4,0},{8,4},{12,8},{16,12},{20,16},{24,20},{28,24},{32,28},{36,32}... | collective-permute-start | bytes 1179656 | tf_op jit(solution)/shard_map/ppermute | solution.py:28
  46.0 9.5 %collective-permute-start.5 = (bf16[3,3,1,2,32,128]{5,4,3,2,1,0:T(8,128)(2,1)S(1)}, bf16[3,3,1,2,32,128]{5,4,3,2,1,0:T(8,128)(2,1)S(1)}, u32[]{:S(2)}, u32[]{:S(2)}) collective-permute-start(bf16[3,3,1,2,32,128]{5,4,3,2,1,0:T(8,128)(2,1)S(1)} %get-tuple-element.10), channel_id=1, source_target_pairs={{0,1},{1,2},{2,3},{3,0},{4,5},{5,6},{6,7},{7,4},{8,9},{9,10},{10,1... | collective-permute-start | bytes 442376 | tf_op jit(solution)/shard_map/ppermute | solution.py:25
  47.9 7.6 %collective-permute-start.4 = (bf16[3,3,1,2,32,128]{5,4,3,2,1,0:T(8,128)(2,1)S(1)}, bf16[3,3,1,2,32,128]{5,4,3,2,1,0:T(8,128)(2,1)S(1)}, u32[]{:S(2)}, u32[]{:S(2)}) collective-permute-start(bf16[3,3,1,2,32,128]{5,4,3,2,1,0:T(8,128)(2,1)S(1)} %get-tuple-element.11), channel_id=1, source_target_pairs={{1,0},{2,1},{3,2},{0,3},{5,4},{6,5},{7,6},{4,7},{9,8},{10,9},{11,1... | collective-permute-start | bytes 442376 | tf_op jit(solution)/shard_map/ppermute | solution.py:28
  55.6 1.0 copy-start.1
  61.9 0.9 copy-start.2
  62.8 2.6 %copy-start.3 = (f32[9]{0:T(128)S(1)}, f32[9]{0:T(128)}, u32[]{:S(2)}) copy-start(f32[9]{0:T(128)} %convert_element_type.51) | copy-start | bytes 112
  68.8 12.7 %collective-permute-start.6 = (f32[4,9,2048]{2,0,1:T(4,128)S(1)}, f32[4,9,2048]{2,0,1:T(4,128)S(1)}, u32[]{:S(2)}, u32[]{:S(2)}) collective-permute-start(f32[4,9,2048]{2,0,1:T(4,128)S(1)} %copy.62), channel_id=1, source_target_pairs={{0,64},{64,0},{128,192},{192,128},{256,320},{320,256},{384,448},{4... | collective-permute-start | bytes 884744 | tf_op jit(solution)/shard_map/ppermute | solution.py:36
Sparse Core Ops, SparseCore 0:
  82.9 104.9 all-gather.2
where the time goes:
time: 205 us; the launch traced here: 204 us
  waiting for transfers between devices  110 us (54%)
  starting transfers between devices  40.4 us (20%)
  local copies, waits for them, and re-layouts  15.9 us (8%)
  between operations  13.7 us (7%)
  matrix products  13.5 us (7%)
  other arithmetic  10.2 us (5%)
    all_gather x1, waiting for transfers between devices, local(): incoming = lax.all_gather(partial_value[None], 'gy', axis=0, tiled=True)  103 us
    ppermute x3, starting transfers between devices, with_halo(): lax.ppermute(lax.slice_in_dim(block, 0, width, axis=dim), axis, backward)  20.7 us
    ppermute x1, starting transfers between devices, partner(): return lax.ppermute(value, axis, pairs)  11.5 us
    dot_general x1, matrix products, local(): jnp.einsum('nqs,nqkf->skf', onehot, incoming, precision=lax.Precision.HIG...  9.17 us
    ppermute x3, starting transfers between devices, with_halo(): lax.ppermute(lax.slice_in_dim(block, block.shape[dim] - width, None, axis...  8.22 us
    unnamed x17, local copies, waits for them, and re-layouts  7.28 us
  transfers between devices with their start and end apart: 8, of which 5 were waited for; matrix products, arithmetic and copies ran while one was open for 7% of the time, Pallas kernels for 0%

commit v1 on v0

v1 whole, which is shorter than its diff:
```python
import jax
import jax.numpy as jnp
from jax import lax
from jax.experimental import pallas as pl
from jax.experimental.pallas import tpu as pltpu
from jax.sharding import Mesh, PartitionSpec as P

F32 = jnp.float32
BF16 = jnp.bfloat16
GX = ("xh", "xl")
GY = ("yl", "yh", "yp")


def swap_inner(count):
    return [(i, i ^ 1) for i in range(count)]


def swap_outer(count):
    pairs = []
    for i in range(count):
        step = 1 if i % 2 else -1
        pairs.append((i, (i + step) % count))
    return pairs


def shift(count, step):
    return [(i, (i + step) % count) for i in range(count)]


def lane_low(shape):
    return lax.broadcasted_iota(jnp.int32, shape, 1) < 64


def block_of(vectors):
    wide = vectors.astype(F32)
    upper = jnp.where(lane_low(wide.shape), wide, -wide)
    lower = pltpu.roll(wide, 64, 1)
    return jnp.concatenate(
        [upper.astype(BF16), lower.astype(BF16), lower.astype(BF16), (-upper).astype(BF16)], 0
    )


def hop(link_block, rows):
    out = lax.dot_general(link_block, rows, (((1,), (1,)), ((), ())), preferred_element_type=F32)
    return out.astype(BF16)


def project(own, stacked):
    return jnp.dot(own, stacked, preferred_element_type=F32)


def fold(result):
    low = lane_low((16, 128))
    first = jnp.where(low, result[0:16], result[48:64])
    second = jnp.where(low, result[16:32], result[32:48])
    return first + pltpu.roll(second, 64, 1)


def hop_kernel(
    off_ref, links_ref, v_ref, xa_ref, xb_ref, ya_ref, yb_ref, zl_ref, zh_ref, out_ref, vf_ref, rows_ref
):
    def find(axis, sign):
        index = jnp.int32(0)
        for k in range(9):
            index = index + jnp.where(off_ref[k, axis] == sign, k, 0).astype(jnp.int32)
        return index

    k_self = jnp.int32(36)
    minus = [find(axis, -1) for axis in range(4)]
    plus = [find(axis, 1) for axis in range(4)]
    for axis in range(4):
        k_self = k_self - minus[axis] - plus[axis]
    x_odd = lax.axis_index("xl") == 1
    y_odd = lax.axis_index("yp") == 1
    x_out = jnp.where(x_odd, plus[0], minus[0])
    x_in = jnp.where(x_odd, minus[0], plus[0])
    y_out = jnp.where(y_odd, plus[1], minus[1])
    y_in = jnp.where(y_odd, minus[1], plus[1])

    for z in range(8):
        for t in range(2):
            vf_ref[pl.ds((2 * z + t) * 32, 32), :] = v_ref[z, t].astype(F32)
            rows_ref[2 * z + t] = block_of(v_ref[z, t])

    low = lane_low((16, 128))
    low_own = lane_low((64, 128))
    zero = jnp.zeros((16, 128), BF16)
    for agg in range(4):
        halves = []
        for zz in range(2):
            base = (2 * (2 * agg + zz)) * 32
            quarter = []
            for first in range(2):
                left = vf_ref[pl.ds(base + first, 16, stride=2), :]
                right = vf_ref[pl.ds(base + 32 + first, 16, stride=2), :]
                quarter.append(
                    (
                        jnp.where(low, left, pltpu.roll(right, 64, 1)),
                        jnp.where(low, pltpu.roll(left, 64, 1), right),
                    )
                )
            half = jnp.concatenate([quarter[0][0], quarter[1][0], quarter[0][1], quarter[1][1]], 0)
            halves.append(half)
        own = jnp.concatenate([h.astype(BF16) for h in halves], 1)
        own_t0 = jnp.concatenate([jnp.where(low_own, h, 0.0).astype(BF16) for h in halves], 1)
        own_t1 = jnp.concatenate([jnp.where(low_own, 0.0, h).astype(BF16) for h in halves], 1)

        sites = [(2 * agg + zz, t) for zz in range(2) for t in range(2)]
        g_self, g_tin, g_tout, g_zin, g_zout = {}, {}, {}, {}, {}
        for z, t in sites:
            k_tin = plus[3] if t == 1 else minus[3]
            k_tout = minus[3] if t == 1 else plus[3]
            k_zin = minus[2] if z % 2 == 0 else plus[2]
            stack = jnp.concatenate(
                [
                    links_ref[z, t, k_self],
                    links_ref[z, 1 - t, k_tin],
                    links_ref[z, 1 - t, k_tout],
                    links_ref[z ^ 1, t, k_zin],
                ],
                0,
            )
            res = hop(stack, rows_ref[2 * z + t])
            g_self[(z, t)] = res[0:64]
            g_tin[(z, 1 - t)] = res[64:128]
            g_tout[(z, 1 - t)] = res[128:192]
            g_zin[(z ^ 1, t)] = res[192:256]
        for z, t in sites:
            if z % 2 == 0:
                k_zout, target = minus[2], z - 1
            else:
                k_zout, target = plus[2], z + 1
            if target < 0:
                rows = block_of(zl_ref[0, t])
            elif target > 7:
                rows = block_of(zh_ref[0, t])
            else:
                rows = rows_ref[2 * target + t]
            g_zout[(z, t)] = hop(links_ref[z, t, k_zout], rows)

        def cat(table):
            return jnp.concatenate([table[s] for s in sites], 0)

        def halo(ref, k):
            return jnp.concatenate([hop(links_ref[z, t, k], block_of(ref[z, t])) for z, t in sites], 0)

        total = project(own, cat(g_self))
        total = total + project(own, cat(g_tin))
        total = total + project(own, cat(g_zin))
        total = total + project(own, halo(xa_ref, x_in))
        total = total + project(own, halo(ya_ref, y_in))
        out_ref[agg, k_self] = fold(total).astype(BF16)
        out_ref[agg, x_out] = fold(project(own, halo(xb_ref, x_out))).astype(BF16)
        out_ref[agg, y_out] = fold(project(own, halo(yb_ref, y_out))).astype(BF16)
        out_ref[agg, x_in] = zero
        out_ref[agg, y_in] = zero
        z_out = cat(g_zout)
        out_ref[agg, minus[2]] = fold(project(own[:, :128], z_out[:128])).astype(BF16)
        out_ref[agg, plus[2]] = fold(project(own[:, 128:], z_out[128:])).astype(BF16)
        t_out = cat(g_tout)
        out_ref[agg, minus[3]] = fold(project(own_t0, t_out)).astype(BF16)
        out_ref[agg, plus[3]] = fold(project(own_t1, t_out)).astype(BF16)


def place_kernel(place_ref, own_ref, other_ref, out_ref, table_ref, wide_ref):
    line = lax.axis_index("xh")
    column = lax.axis_index("xl")
    block = lax.axis_index("gz")

    def note(entry, carry):
        cy = entry // 4
        target = place_ref[line, cy, block * 4 + entry % 4]
        table_ref[target] = entry
        return carry

    lax.fori_loop(0, 32, note, 0, unroll=True)

    def emit(slot, carry):
        entry = table_ref[column * 16 + slot]
        source = 2 * (entry // 4) + entry % 2
        is_own = (entry % 4) // 2 == column
        wide_ref[...] = jnp.where(
            is_own, own_ref[source].astype(F32), other_ref[source].astype(F32)
        ).reshape(144, 128)
        for lane in range(16):
            out_ref[slot, :, lane * 128 : (lane + 1) * 128] = wide_ref[pl.ds(lane, 9, stride=16), :]
        return carry

    lax.fori_loop(0, 16, emit, 0)


def local(links, null_vectors, offsets, place):
    own = null_vectors[0, 0]
    links = links[0, 0]
    z_low = lax.ppermute(own[7:8], "gz", shift(4, 1))
    z_high = lax.ppermute(own[0:1], "gz", shift(4, -1))
    x_inner = lax.ppermute(own, "xl", swap_inner(2))
    x_outer = lax.ppermute(own, GX, swap_outer(16))
    y_inner = lax.ppermute(own, "yp", swap_inner(2))
    y_outer = lax.ppermute(own, GY, swap_outer(16))
    vmem = pl.BlockSpec(memory_space=pltpu.VMEM)
    smem = pl.BlockSpec(memory_space=pltpu.SMEM)
    partial_value = pl.pallas_call(
        hop_kernel,
        out_shape=jax.ShapeDtypeStruct((4, 9, 16, 128), BF16),
        in_specs=[smem] + [vmem] * 8,
        out_specs=vmem,
        scratch_shapes=[pltpu.VMEM((512, 128), F32), pltpu.VMEM((16, 128, 128), BF16)],
        compiler_params=pltpu.CompilerParams(vmem_limit_bytes=32 * 1024 * 1024),
        cost_estimate=pl.CostEstimate(flops=300_000_000, bytes_accessed=4_000_000, transcendentals=0),
        name="hop",
    )(offsets, links, own, x_inner, x_outer, y_inner, y_outer, z_low, z_high)
    parts = lax.all_to_all(partial_value, ("xl", "yp"), 0, 0, tiled=True)
    chunk = jnp.sum(parts.astype(F32), axis=0).astype(BF16)
    spread = jnp.broadcast_to(chunk[None], (16, 9, 16, 128))
    mine = lax.all_to_all(spread, GY, 0, 0, tiled=True)
    other = lax.ppermute(mine, "xl", swap_inner(2))
    placed = pl.pallas_call(
        place_kernel,
        out_shape=jax.ShapeDtypeStruct((16, 9, 2048), F32),
        in_specs=[smem, vmem, vmem],
        out_specs=vmem,
        scratch_shapes=[pltpu.SMEM((32,), jnp.int32), pltpu.VMEM((144, 128), F32)],
        compiler_params=pltpu.CompilerParams(vmem_limit_bytes=32 * 1024 * 1024),
        name="place",
    )(place.reshape(8, 8, 16), mine, other)
    return placed[None, None]


def solution(mesh):
    fine = Mesh(mesh.devices.reshape(8, 2, 2, 4, 2, 4), ("xh", "xl", "yl", "yh", "yp", "gz"))
    placed = (P(GX, GY, "gz"), P(GX, GY, "gz"), P(), P())
    return jax.shard_map(
        local,
        mesh=fine,
        in_specs=placed,
        out_specs=P(GX, "gz"),
        check_vma=False,
    )
```

time: 205 us -> 90.8 us (0.44)
  waiting for transfers between devices: 110 us -> 3.42 us
  blocking collectives: 0 us -> 30.4 us
  between operations: 13.7 us -> 0.1 us
  matrix products: 13.5 us -> 0 us
  other arithmetic: 10.2 us -> 0.02 us
  local copies, waits for them, and re-layouts: 15.9 us -> 5.86 us
  Pallas kernels: 0 us -> 7.29 us
  starting transfers between devices: 40.4 us -> 43.2 us
    all_gather x1 -> x0, waiting for transfers between devices: 103 us -> none  [local(): incoming = lax.all_gather(partial_value[None], 'gy', axis=0, tiled=True)]
    all_to_all x0 -> x2, blocking collectives: none -> 30.4 us  [the longest x1 21.3 us: local(): mine = lax.all_to_all(spread, GY, 0, 0, tiled=True)]
    dot_general x3 -> x0, matrix products: 13.5 us -> none  [the longest x1 9.17 us: local(): jnp.einsum('nqs,nqkf->skf', onehot, incoming, precision=lax.Precision.HIG...]
    pallas_call x0 -> x2, Pallas kernels: none -> 7.29 us  [the longest x1 5.25 us: local(): pl.pallas_call(hop_kernel, out_shape=jax.ShapeDtypeStruct((4, 9, 16, 128)...]
    unnamed x17 -> x7, local copies, waits for them, and re-layouts: 7.28 us -> 3.34 us
    ppermute x7, waiting for transfers between devices: 6.62 us -> 3.42 us  [the longest x1 1.61 us: local(): other = lax.ppermute(mine, 'xl', swap_inner(2))]
    gather x3 -> x0, local copies, waits for them, and re-layouts: 2.93 us -> none  [the longest x1 2.16 us: local(): neighbour = jnp.take(stacked, chosen, axis=0)]
    ppermute x7, starting transfers between devices: 40.4 us -> 43.2 us  [the longest x1 13.6 us: local(): x_inner = lax.ppermute(own, 'xl', swap_inner(2))]
  transfers between devices with their start and end apart: 8 -> 7, of which waited for: 5 -> 3; matrix products, arithmetic and copies ran while one was open for 7% -> 2% of each run, Pallas kernels for 0% -> 0%
where the time goes in v1:
time: 90.8 us; the launch traced here: 90.3 us
  starting transfers between devices  43.2 us (48%)
  blocking collectives  30.4 us (33%)
  Pallas kernels  7.29 us (8%)
  local copies, waits for them, and re-layouts  5.86 us (6%)
  waiting for transfers between devices  3.42 us (4%)
    all_to_all x1, blocking collectives, local(): mine = lax.all_to_all(spread, GY, 0, 0, tiled=True)  21.3 us
    ppermute x1, starting transfers between devices, local(): x_inner = lax.ppermute(own, 'xl', swap_inner(2))  13.6 us
    all_to_all x1, blocking collectives, local(): parts = lax.all_to_all(partial_value, ('xl', 'yp'), 0, 0, tiled=True)  9.13 us
    ppermute x1, starting transfers between devices, local(): y_outer = lax.ppermute(own, GY, swap_outer(16))  6.43 us
    ppermute x1, starting transfers between devices, local(): x_outer = lax.ppermute(own, GX, swap_outer(16))  5.75 us
    ppermute x1, starting transfers between devices, local(): z_high = lax.ppermute(own[0:1], 'gz', shift(4, -1))  5.65 us
    pallas_call x1, Pallas kernels, local(): pl.pallas_call(hop_kernel, out_shape=jax.ShapeDtypeStruct((4, 9, 16, 128)...  5.25 us
    ppermute x1, starting transfers between devices, local(): z_low = lax.ppermute(own[7:8], 'gz', shift(4, 1))  5.11 us
  transfers between devices with their start and end apart: 7, of which 3 were waited for; matrix products, arithmetic and copies ran while one was open for 2% of the time, Pallas kernels for 0%

profile of v1, /device:TPU:1, one launch (start us, length us, event | category | flops | bytes accessed | tf_op | source)
XLA Modules:
  0.0 90.3 jit_solution(179081144219191583)
XLA Ops:
  0.0 6.4 %collective-permute-start.3 = (bf16[8,2,32,128]{3,2,1,0:T(8,128)(2,1)}, bf16[8,2,32,128]{3,2,1,0:T(8,128)(2,1)S(1)}, u32[]{:S(2)}, u32[]{:S(2)}) collective-permute-start(bf16[8,2,32,128]{3,2,1,0:T(8,128)(2,1)} %bitcast.10), channel_id=1, source_target_pairs={{0,60},{4,8},{8,4},{12,16},{16,12},{20,24},{24,20},{28,32},{32,28}... | collective-permute-start | bytes 393224 | tf_op jit(solution)/shard_map/ppermute | solution.py:200
  6.4 1.9 %collective-permute-start.2 = (bf16[8,2,32,128]{3,2,1,0:T(8,128)(2,1)}, bf16[8,2,32,128]{3,2,1,0:T(8,128)(2,1)S(1)}, u32[]{:S(2)}, u32[]{:S(2)}) collective-permute-start(bf16[8,2,32,128]{3,2,1,0:T(8,128)(2,1)} %bitcast.11), channel_id=1, source_target_pairs={{0,4},{4,0},{1,5},{5,1},{2,6},{6,2},{3,7},{7,3},{8,12},{12,8},{9,1... | collective-permute-start | bytes 393224 | tf_op jit(solution)/shard_map/ppermute | solution.py:199
  8.4 5.8 %collective-permute-start.1 = (bf16[8,2,32,128]{3,2,1,0:T(8,128)(2,1)}, bf16[8,2,32,128]{3,2,1,0:T(8,128)(2,1)S(1)}, u32[]{:S(2)}, u32[]{:S(2)}) collective-permute-start(bf16[8,2,32,128]{3,2,1,0:T(8,128)(2,1)} %bitcast.12), channel_id=1, source_target_pairs={{0,960},{64,128},{128,64},{192,256},{256,192},{320,384},{384,320},... | collective-permute-start | bytes 393224 | tf_op jit(solution)/shard_map/ppermute | solution.py:198
  14.1 13.6 %collective-permute-start = (bf16[8,2,32,128]{3,2,1,0:T(8,128)(2,1)}, bf16[8,2,32,128]{3,2,1,0:T(8,128)(2,1)S(1)}, u32[]{:S(2)}, u32[]{:S(2)}) collective-permute-start(bf16[8,2,32,128]{3,2,1,0:T(8,128)(2,1)} %bitcast.13), channel_id=1, source_target_pairs={{0,64},{64,0},{1,65},{65,1},{2,66},{66,2},{3,67},{67,3},{4,68},{68... | collective-permute-start | bytes 393224 | tf_op jit(solution)/shard_map/ppermute | solution.py:197
  27.7 0.7 slice_bitcast_fusion
  28.5 5.7 %collective-permute-start.5 = (bf16[1,2,32,128]{3,2,1,0:T(8,128)(2,1)S(1)}, bf16[1,2,32,128]{3,2,1,0:T(8,128)(2,1)S(1)}, u32[]{:S(2)}, u32[]{:S(2)}) collective-permute-start(bf16[1,2,32,128]{3,2,1,0:T(8,128)(2,1)S(1)} %get-tuple-element.5), channel_id=1, source_target_pairs={{0,3},{1,0},{2,1},{3,2},{4,7},{5,4},{6,5},{7,6},{8,11},{9,8},{10,9... | collective-permute-start | bytes 49160 | tf_op jit(solution)/shard_map/ppermute | solution.py:196
  34.1 0.8 collective-permute-done.5.zh_ref
  35.0 5.1 %collective-permute-start.4 = (bf16[1,2,32,128]{3,2,1,0:T(8,128)(2,1)S(1)}, bf16[1,2,32,128]{3,2,1,0:T(8,128)(2,1)S(1)}, u32[]{:S(2)}, u32[]{:S(2)}) collective-permute-start(bf16[1,2,32,128]{3,2,1,0:T(8,128)(2,1)S(1)} %get-tuple-element.6), channel_id=1, source_target_pairs={{0,1},{1,2},{2,3},{3,0},{4,5},{5,6},{6,7},{7,4},{8,9},{9,10},{10,1... | collective-permute-start | bytes 49160 | tf_op jit(solution)/shard_map/ppermute | solution.py:195
  40.1 0.8 copy.5.off_ref
  40.9 1.0 %collective-permute-done.4.zl_ref = bf16[1,2,32,128]{3,2,1,0:T(8,128)(2,1)S(1)} collective-permute-done((bf16[1,2,32,128]{3,2,1,0:T(8,128)(2,1)S(1)}, bf16[1,2,32,128]{3,2,1,0:T(8,128)(2,1)S(1)}, u32[]{:S(2)}, u32[]{:S(2)}) %collective-permute-start.4) | collective-permute-done | bytes 16416 | tf_op jit(solution)/shard_map/ppermute | solution.py:195
  41.8 0.0 collective-permute-done.3.yb_ref
  41.8 0.0 collective-permute-done.2.ya_ref
  41.8 0.0 collective-permute-done.1.xb_ref
  41.8 0.0 collective-permute-done.xa_ref
  41.9 0.0 copy-start
  41.9 1.7 %copy-done = bf16[1,1,8,2,9,64,128]{6,5,4,3,2,1,0:T(8,128)(2,1)S(1)} copy-done((bf16[1,1,8,2,9,64,128]{6,5,4,3,2,1,0:T(8,128)(2,1)S(1)}, bf16[1,1,8,2,9,64,128]{6,5,4,3,2,1,0:T(8,128)(2,1)}, u32[]{:S(2)}) %copy-start) | copy-done | bytes 2359320
  43.5 0.0 copy-start.1
  43.5 0.9 copy-done.1
  44.4 0.0 copy-start.2
  44.4 5.2 %hop.1 = bf16[4,9,16,128]{3,2,1,0:T(8,128)(2,1)S(1)} custom-call(s32[9,4]{1,0:T(8,128)S(1)} %copy.5.off_ref, bf16[8,2,9,64,128]{4,3,2,1,0:T(8,128)(2,1)S(1)} %bitcast.9, bf16[8,2,32,128]{3,2,1,0:T(8,128)(2,1)S(1)} %bitcast.14, bf16[8,2,32,128]{3,2,1,0:T(8,128)(2,1)S(1)} %collective-permute-done.xa_ref, ...), custom_call_target="tpu_custom_call" | custom-call | flops 300000000 | bytes 4000000 | tf_op jit(solution)/shard_map/hop/pallas_call | solution.py:203
  49.7 9.1 %all_to_all.10 = bf16[4,9,16,128]{3,2,1,0:T(8,128)(2,1)S(1)} all-to-all(bf16[4,9,16,128]{3,2,1,0:T(8,128)(2,1)S(1)} %hop.1), channel_id=1, replica_groups=mesh['xh'=8,'xl'=2,'yl'=2,'yh'=4,'yp'=2,'gz'=4] {'xl','yp'}, dimensions={0} | all-to-all | bytes 294912 | tf_op jit(solution)/shard_map/all_to_all | solution.py:213
  58.8 0.1 broadcast_in_dim.4
  58.9 21.3 %all_to_all.11.own_ref = bf16[16,9,16,128]{3,2,1,0:T(8,128)(2,1)S(1)} all-to-all(bf16[16,9,16,128]{3,2,1,0:T(8,128)(2,1)S(1)} %broadcast_in_dim.4), channel_id=1, replica_groups=mesh['xh'=8,'xl'=2,'yl'=2,'yh'=4,'yp'=2,'gz'=4] {'yl','yh','yp'}, dimensions={0} | all-to-all | bytes 1179648 | tf_op jit(solution)/shard_map/all_to_all | solution.py:216
  80.2 4.7 %collective-permute-start.6 = (bf16[16,9,16,128]{3,2,1,0:T(8,128)(2,1)S(1)}, bf16[16,9,16,128]{3,2,1,0:T(8,128)(2,1)S(1)}, u32[]{:S(2)}, u32[]{:S(2)}) collective-permute-start(bf16[16,9,16,128]{3,2,1,0:T(8,128)(2,1)S(1)} %all_to_all.11.own_ref), channel_id=1, source_target_pairs={{0,64},{64,0},{1,65},{65,1},{2,66},{66,2},{3,67},{67,3},{4,68},{68... | collective-permute-start | bytes 1769480 | tf_op jit(solution)/shard_map/ppermute | solution.py:217
  84.9 1.6 %collective-permute-done.6.other_ref = bf16[16,9,16,128]{3,2,1,0:T(8,128)(2,1)S(1)} collective-permute-done((bf16[16,9,16,128]{3,2,1,0:T(8,128)(2,1)S(1)}, bf16[16,9,16,128]{3,2,1,0:T(8,128)(2,1)S(1)}, u32[]{:S(2)}, u32[]{:S(2)}) %collective-permute-start.6) | collective-permute-done | bytes 589856 | tf_op jit(solution)/shard_map/ppermute | solution.py:217
  86.5 0.0 copy-done.2
  86.5 2.0 %place.1 = f32[16,9,2048]{2,1,0:T(8,128)S(1)} custom-call(s32[8,8,16]{2,1,0:T(8,128)S(1)} %bitcast.15, bf16[16,9,16,128]{3,2,1,0:T(8,128)(2,1)S(1)} %all_to_all.11.own_ref, bf16[16,9,16,128]{3,2,1,0:T(8,128)(2,1)S(1)} %collective-permute-done.6.other_ref), custom_call_target="tpu_custom_call" | custom-call | tf_op jit(solution)/shard_map/place/pallas_call | solution.py:218
  88.6 1.7 %copy.6 = f32[1,1,16,9,2048]{4,2,3,1,0:T(8,128)} copy(f32[1,1,16,9,2048]{4,3,2,1,0:T(8,128)S(1)} %bitcast.8) | data formatting | bytes 2359296 | tf_op jit(solution)/shard_map/broadcast_in_dim | solution.py:227
  (1 shorter events, 0.0 us)
Async XLA Ops:
  0.0 41.8 %collective-permute-start.3 = (bf16[8,2,32,128]{3,2,1,0:T(8,128)(2,1)}, bf16[8,2,32,128]{3,2,1,0:T(8,128)(2,1)S(1)}, u32[]{:S(2)}, u32[]{:S(2)}) collective-permute-start(bf16[8,2,32,128]{3,2,1,0:T(8,128)(2,1)} %bitcast.10), channel_id=1, source_target_pairs={{0,60},{4,8},{8,4},{12,16},{16,12},{20,24},{24,20},{28,32},{32,28}... | collective-permute-start | bytes 393224 | tf_op jit(solution)/shard_map/ppermute | solution.py:200
  6.4 35.4 %collective-permute-start.2 = (bf16[8,2,32,128]{3,2,1,0:T(8,128)(2,1)}, bf16[8,2,32,128]{3,2,1,0:T(8,128)(2,1)S(1)}, u32[]{:S(2)}, u32[]{:S(2)}) collective-permute-start(bf16[8,2,32,128]{3,2,1,0:T(8,128)(2,1)} %bitcast.11), channel_id=1, source_target_pairs={{0,4},{4,0},{1,5},{5,1},{2,6},{6,2},{3,7},{7,3},{8,12},{12,8},{9,1... | collective-permute-start | bytes 393224 | tf_op jit(solution)/shard_map/ppermute | solution.py:199
  8.4 33.5 %collective-permute-start.1 = (bf16[8,2,32,128]{3,2,1,0:T(8,128)(2,1)}, bf16[8,2,32,128]{3,2,1,0:T(8,128)(2,1)S(1)}, u32[]{:S(2)}, u32[]{:S(2)}) collective-permute-start(bf16[8,2,32,128]{3,2,1,0:T(8,128)(2,1)} %bitcast.12), channel_id=1, source_target_pairs={{0,960},{64,128},{128,64},{192,256},{256,192},{320,384},{384,320},... | collective-permute-start | bytes 393224 | tf_op jit(solution)/shard_map/ppermute | solution.py:198
  14.1 27.7 %collective-permute-start = (bf16[8,2,32,128]{3,2,1,0:T(8,128)(2,1)}, bf16[8,2,32,128]{3,2,1,0:T(8,128)(2,1)S(1)}, u32[]{:S(2)}, u32[]{:S(2)}) collective-permute-start(bf16[8,2,32,128]{3,2,1,0:T(8,128)(2,1)} %bitcast.13), channel_id=1, source_target_pairs={{0,64},{64,0},{1,65},{65,1},{2,66},{66,2},{3,67},{67,3},{4,68},{68... | collective-permute-start | bytes 393224 | tf_op jit(solution)/shard_map/ppermute | solution.py:197
  28.5 6.5 %collective-permute-start.5 = (bf16[1,2,32,128]{3,2,1,0:T(8,128)(2,1)S(1)}, bf16[1,2,32,128]{3,2,1,0:T(8,128)(2,1)S(1)}, u32[]{:S(2)}, u32[]{:S(2)}) collective-permute-start(bf16[1,2,32,128]{3,2,1,0:T(8,128)(2,1)S(1)} %get-tuple-element.5), channel_id=1, source_target_pairs={{0,3},{1,0},{2,1},{3,2},{4,7},{5,4},{6,5},{7,6},{8,11},{9,8},{10,9... | collective-permute-start | bytes 49160 | tf_op jit(solution)/shard_map/ppermute | solution.py:196
  35.0 6.8 %collective-permute-start.4 = (bf16[1,2,32,128]{3,2,1,0:T(8,128)(2,1)S(1)}, bf16[1,2,32,128]{3,2,1,0:T(8,128)(2,1)S(1)}, u32[]{:S(2)}, u32[]{:S(2)}) collective-permute-start(bf16[1,2,32,128]{3,2,1,0:T(8,128)(2,1)S(1)} %get-tuple-element.6), channel_id=1, source_target_pairs={{0,1},{1,2},{2,3},{3,0},{4,5},{5,6},{6,7},{7,4},{8,9},{9,10},{10,1... | collective-permute-start | bytes 49160 | tf_op jit(solution)/shard_map/ppermute | solution.py:195
  41.9 1.7 %copy-start = (bf16[1,1,8,2,9,64,128]{6,5,4,3,2,1,0:T(8,128)(2,1)S(1)}, bf16[1,1,8,2,9,64,128]{6,5,4,3,2,1,0:T(8,128)(2,1)}, u32[]{:S(2)}) copy-start(bf16[1,1,8,2,9,64,128]{6,5,4,3,2,1,0:T(8,128)(2,1)} %param.4) | copy-start | bytes 7077892
  43.5 0.9 %copy-start.1 = (bf16[1,1,8,2,32,128]{5,4,3,2,1,0:T(8,128)(2,1)S(1)}, bf16[1,1,8,2,32,128]{5,4,3,2,1,0:T(8,128)(2,1)}, u32[]{:S(2)}) copy-start(bf16[1,1,8,2,32,128]{5,4,3,2,1,0:T(8,128)(2,1)} %param.5) | copy-start | bytes 393220
  44.4 42.1 %copy-start.2 = (s32[8,8,16,1]{2,3,1,0:T(1,128)S(1)}, s32[8,8,16,1]{2,3,1,0:T(1,128)}, u32[]{:S(2)}) copy-start(s32[8,8,16,1]{2,3,1,0:T(1,128)} %param.7) | copy-start | bytes 12292
  80.2 6.3 %collective-permute-start.6 = (bf16[16,9,16,128]{3,2,1,0:T(8,128)(2,1)S(1)}, bf16[16,9,16,128]{3,2,1,0:T(8,128)(2,1)S(1)}, u32[]{:S(2)}, u32[]{:S(2)}) collective-permute-start(bf16[16,9,16,128]{3,2,1,0:T(8,128)(2,1)S(1)} %all_to_all.11.own_ref), channel_id=1, source_target_pairs={{0,64},{64,0},{1,65},{65,1},{2,66},{66,2},{3,67},{67,3},{4,68},{68... | collective-permute-start | bytes 1769480 | tf_op jit(solution)/shard_map/ppermute | solution.py:217

commit v2 on v1

v2 whole, which is shorter than its diff:
```python
import jax
import jax.numpy as jnp
from jax import lax
from jax.experimental import pallas as pl
from jax.experimental.pallas import tpu as pltpu
from jax.sharding import Mesh, PartitionSpec as P

F32 = jnp.float32
BF16 = jnp.bfloat16
GX = ("xh", "xl")
GY = ("yl", "yh", "yp")


def swap_inner(count):
    return [(i, i ^ 1) for i in range(count)]


def swap_outer(count):
    pairs = []
    for i in range(count):
        step = 1 if i % 2 else -1
        pairs.append((i, (i + step) % count))
    return pairs


def shift(count, step):
    return [(i, (i + step) % count) for i in range(count)]


def lane_index(shape):
    return lax.broadcasted_iota(jnp.int32, shape, 1)


def block_of(vectors):
    wide = vectors.astype(F32)
    upper = jnp.where(lane_index(wide.shape) < 64, wide, -wide)
    lower = pltpu.roll(wide, 64, 1)
    return jnp.concatenate([upper.astype(BF16), lower.astype(BF16)], 0)


def hop(link_block, rows):
    out = lax.dot_general(link_block, rows, (((1,), (1,)), ((), ())), preferred_element_type=F32)
    return out.astype(BF16)


def project(own, stacked):
    return jnp.dot(own, stacked, preferred_element_type=F32)


def fold(result):
    first = jnp.concatenate([result[0:16], result[16:32]], 1)
    second = jnp.concatenate([result[32:48], result[48:64]], 1)
    low = lane_index((16, 128)) % 64 < 32
    return first + jnp.where(low, pltpu.roll(second, 96, 1), -pltpu.roll(second, 32, 1))


def roles_of(off_ref):
    def find(axis, sign):
        index = jnp.int32(0)
        for k in range(9):
            index = index + jnp.where(off_ref[axis, k] == sign, k, 0).astype(jnp.int32)
        return index

    minus = [find(axis, -1) for axis in range(4)]
    plus = [find(axis, 1) for axis in range(4)]
    k_self = jnp.int32(36)
    for axis in range(4):
        k_self = k_self - minus[axis] - plus[axis]
    return k_self, minus, plus


def sites_of(agg):
    return [(2 * agg + zz, t) for zz in range(2) for t in range(2)]


def inside_kernel(off_ref, links_ref, v_ref, part_ref, acc_ref, own_ref, vf_ref, rows_ref):
    k_self, minus, plus = roles_of(off_ref)
    for z in range(8):
        for t in range(2):
            vf_ref[pl.ds((2 * z + t) * 32, 32), :] = v_ref[z, t].astype(F32)
            rows_ref[2 * z + t] = block_of(v_ref[z, t])

    low = lane_index((16, 128)) < 64
    low_own = lane_index((64, 128)) < 64
    for agg in range(4):
        halves = []
        for zz in range(2):
            base = (2 * (2 * agg + zz)) * 32
            quarter = []
            for first in range(2):
                left = vf_ref[pl.ds(base + first, 16, stride=2), :]
                right = vf_ref[pl.ds(base + 32 + first, 16, stride=2), :]
                quarter.append(
                    (
                        jnp.where(low, left, pltpu.roll(right, 64, 1)),
                        jnp.where(low, pltpu.roll(left, 64, 1), right),
                    )
                )
            half = jnp.concatenate([quarter[0][0], quarter[1][0], quarter[0][1], quarter[1][1]], 0)
            halves.append(half)
        own = jnp.concatenate([h.astype(BF16) for h in halves], 1)
        own_ref[agg] = own
        own_t0 = jnp.concatenate([jnp.where(low_own, h, 0.0).astype(BF16) for h in halves], 1)
        own_t1 = jnp.concatenate([jnp.where(low_own, 0.0, h).astype(BF16) for h in halves], 1)

        sites = sites_of(agg)
        g_self, g_tin, g_tout, g_zin = {}, {}, {}, {}
        for z, t in sites:
            k_tin = plus[3] if t == 1 else minus[3]
            k_tout = minus[3] if t == 1 else plus[3]
            k_zin = minus[2] if z % 2 == 0 else plus[2]
            stack = jnp.concatenate(
                [
                    links_ref[z, t, k_self],
                    links_ref[z, 1 - t, k_tin],
                    links_ref[z, 1 - t, k_tout],
                    links_ref[z ^ 1, t, k_zin],
                ],
                0,
            )
            res = hop(stack, rows_ref[2 * z + t])
            g_self[(z, t)] = res[0:64]
            g_tin[(z, 1 - t)] = res[64:128]
            g_tout[(z, 1 - t)] = res[128:192]
            g_zin[(z ^ 1, t)] = res[192:256]

        def cat(table):
            return jnp.concatenate([table[s] for s in sites], 0)

        inner = [cat(g_self), cat(g_tin), cat(g_zin)]
        acc_ref[agg] = project(jnp.concatenate([own] * 3, 1), jnp.concatenate(inner, 0))
        t_out = cat(g_tout)
        part_ref[agg, 0] = fold(project(own_t0, t_out)).astype(BF16)
        part_ref[agg, 1] = fold(project(own_t1, t_out)).astype(BF16)
        if agg > 0:
            z = 2 * agg
            down = [hop(links_ref[z, t, minus[2]], rows_ref[2 * (z - 1) + t]) for t in range(2)]
            part_ref[agg, 2] = fold(project(own[:, :128], jnp.concatenate(down, 0))).astype(BF16)
        if agg < 3:
            z = 2 * agg + 1
            up = [hop(links_ref[z, t, plus[2]], rows_ref[2 * (z + 1) + t]) for t in range(2)]
            part_ref[agg, 3] = fold(project(own[:, 128:], jnp.concatenate(up, 0))).astype(BF16)
    part_ref[0, 2] = jnp.zeros((16, 128), BF16)
    part_ref[3, 3] = jnp.zeros((16, 128), BF16)


def across_kernel(
    off_ref,
    links_ref,
    xa_ref,
    xb_ref,
    ya_ref,
    yb_ref,
    zl_ref,
    zh_ref,
    part_ref,
    acc_ref,
    own_ref,
    out_ref,
):
    k_self, minus, plus = roles_of(off_ref)
    x_odd = lax.axis_index("xl") == 1
    y_odd = lax.axis_index("yp") == 1
    x_out = jnp.where(x_odd, plus[0], minus[0])
    x_in = jnp.where(x_odd, minus[0], plus[0])
    y_out = jnp.where(y_odd, plus[1], minus[1])
    y_in = jnp.where(y_odd, minus[1], plus[1])
    zero = jnp.zeros((16, 128), BF16)
    for agg in range(4):
        own = own_ref[agg]
        sites = sites_of(agg)

        def halo(ref, k):
            return jnp.concatenate([hop(links_ref[z, t, k], block_of(ref[z, t])) for z, t in sites], 0)

        inner = jnp.concatenate([halo(xa_ref, x_in), halo(ya_ref, y_in)], 0)
        total = acc_ref[agg] + project(jnp.concatenate([own] * 2, 1), inner)
        out_ref[agg, k_self] = fold(total).astype(BF16)
        out_ref[agg, x_out] = fold(project(own, halo(xb_ref, x_out))).astype(BF16)
        out_ref[agg, y_out] = fold(project(own, halo(yb_ref, y_out))).astype(BF16)
        out_ref[agg, x_in] = zero
        out_ref[agg, y_in] = zero
        out_ref[agg, minus[3]] = part_ref[agg, 0]
        out_ref[agg, plus[3]] = part_ref[agg, 1]
        if agg > 0:
            out_ref[agg, minus[2]] = part_ref[agg, 2]
        else:
            down = [hop(links_ref[0, t, minus[2]], block_of(zl_ref[0, t])) for t in range(2)]
            out_ref[agg, minus[2]] = fold(project(own[:, :128], jnp.concatenate(down, 0))).astype(BF16)
        if agg < 3:
            out_ref[agg, plus[2]] = part_ref[agg, 3]
        else:
            up = [hop(links_ref[7, t, plus[2]], block_of(zh_ref[0, t])) for t in range(2)]
            out_ref[agg, plus[2]] = fold(project(own[:, 128:], jnp.concatenate(up, 0))).astype(BF16)


def place_kernel(place_ref, own_ref, other_ref, out_ref, table_ref, wide_ref, buf_ref, sems):
    line = lax.axis_index("xh")
    column = lax.axis_index("xl")
    block = lax.axis_index("gz")

    for entry in range(32):
        target = place_ref[line, entry // 4, block * 4 + entry % 4]
        table_ref[target] = jnp.int32(entry)

    def gather(slot, carry):
        entry = table_ref[column * 16 + slot]
        source = 2 * (entry // 4) + entry % 2
        is_own = (entry % 4) // 2 == column
        rows = pl.ds(pl.multiple_of(slot * 16, 16), 16)
        for k in range(9):
            picked = jnp.where(is_own, own_ref[source, k].astype(F32), other_ref[source, k].astype(F32))
            wide_ref[k, rows, :] = picked
        return carry

    lax.fori_loop(0, 16, gather, 0, unroll=4)
    copies = []
    for k in range(9):
        for lane in range(16):
            buf_ref[k, :, lane * 128 : (lane + 1) * 128] = wide_ref[k, pl.ds(lane, 16, stride=16), :]
        copies.append(pltpu.make_async_copy(buf_ref.at[k], out_ref.at[k], sems.at[k]))
        copies[k].start()
    for copy in copies:
        copy.wait()


def local(links, null_vectors, offsets, place):
    own = null_vectors[0, 0]
    links = links[0, 0]
    z_low = lax.ppermute(own[7:8], "gz", shift(4, 1))
    z_high = lax.ppermute(own[0:1], "gz", shift(4, -1))
    x_inner = lax.ppermute(own, "xl", swap_inner(2))
    x_outer = lax.ppermute(own, GX, swap_outer(16))
    y_inner = lax.ppermute(own, "yp", swap_inner(2))
    y_outer = lax.ppermute(own, GY, swap_outer(16))
    vmem = pl.BlockSpec(memory_space=pltpu.VMEM)
    smem = pl.BlockSpec(memory_space=pltpu.SMEM)
    anywhere = pl.BlockSpec(memory_space=pl.ANY)
    roles = offsets.T
    part, acc, packed = pl.pallas_call(
        inside_kernel,
        out_shape=(
            jax.ShapeDtypeStruct((4, 4, 16, 128), BF16),
            jax.ShapeDtypeStruct((4, 64, 64), F32),
            jax.ShapeDtypeStruct((4, 64, 256), BF16),
        ),
        in_specs=[smem, vmem, vmem],
        out_specs=(vmem, vmem, vmem),
        scratch_shapes=[pltpu.VMEM((512, 128), F32), pltpu.VMEM((16, 64, 128), BF16)],
        compiler_params=pltpu.CompilerParams(vmem_limit_bytes=16 * 1024 * 1024),
        cost_estimate=pl.CostEstimate(flops=150_000_000, bytes_accessed=3_000_000, transcendentals=0),
        name="inside",
    )(roles, links, own)
    partial_value = pl.pallas_call(
        across_kernel,
        out_shape=jax.ShapeDtypeStruct((4, 9, 16, 128), BF16),
        in_specs=[smem] + [vmem] * 10,
        out_specs=vmem,
        compiler_params=pltpu.CompilerParams(vmem_limit_bytes=16 * 1024 * 1024),
        cost_estimate=pl.CostEstimate(flops=150_000_000, bytes_accessed=3_000_000, transcendentals=0),
        name="across",
    )(roles, links, x_inner, x_outer, y_inner, y_outer, z_low, z_high, part, acc, packed)
    parts = lax.all_to_all(partial_value, ("xl", "yp"), 0, 0, tiled=True)
    chunk = jnp.sum(parts.astype(F32), axis=0).astype(BF16)
    spread = jnp.broadcast_to(chunk[None], (16, 9, 16, 128))
    mine = lax.all_to_all(spread, GY, 0, 0, tiled=True)
    other = lax.ppermute(mine, "xl", swap_inner(2))
    placed = pl.pallas_call(
        place_kernel,
        out_shape=jax.ShapeDtypeStruct((9, 16, 2048), F32),
        in_specs=[smem, vmem, vmem],
        out_specs=anywhere,
        scratch_shapes=[
            pltpu.SMEM((32,), jnp.int32),
            pltpu.VMEM((9, 256, 128), F32),
            pltpu.VMEM((9, 16, 2048), F32),
            pltpu.SemaphoreType.DMA((9,)),
        ],
        compiler_params=pltpu.CompilerParams(vmem_limit_bytes=32 * 1024 * 1024),
        name="place",
    )(place.reshape(8, 8, 16), mine, other)
    return jnp.transpose(placed, (1, 0, 2))[None, None]


def solution(mesh):
    fine = Mesh(mesh.devices.reshape(8, 2, 2, 4, 2, 4), ("xh", "xl", "yl", "yh", "yp", "gz"))
    placed = (P(GX, GY, "gz"), P(GX, GY, "gz"), P(), P())
    return jax.shard_map(
        local,
        mesh=fine,
        in_specs=placed,
        out_specs=P(GX, "gz"),
        check_vma=False,
    )
```

time: 90.8 us -> 88.2 us (0.971)
  local copies, waits for them, and re-layouts: 5.86 us -> 4.07 us
  Pallas kernels: 7.29 us -> 8.59 us
  blocking collectives: 30.4 us -> 29.2 us
  waiting for transfers between devices: 3.42 us -> 2.47 us
    broadcast_in_dim x1 -> x0, local copies, waits for them, and re-layouts: 1.7 us -> none  [local(): return placed[None, None]]
    pallas_call x2 -> x3, Pallas kernels: 7.29 us -> 8.59 us  [the longest x1 3.32 us: local(): pl.pallas_call(across_kernel, out_shape=jax.ShapeDtypeStruct((4, 9, 16, 1...]
    all_to_all x1, blocking collectives: 9.13 us -> 7.93 us  [local(): parts = lax.all_to_all(partial_value, ('xl', 'yp'), 0, 0, tiled=True)]
    ppermute x1, waiting for transfers between devices: 0.95 us -> 0.01 us  [local(): z_low = lax.ppermute(own[7:8], 'gz', shift(4, 1))]
    unnamed x7 -> x8, local copies, waits for them, and re-layouts: 3.34 us -> 3.25 us
  transfers between devices with their start and end apart: 7 -> 7, of which waited for: 3 -> 2; matrix products, arithmetic and copies ran while one was open for 2% -> 1% of each run, Pallas kernels for 0% -> 3%
where the time goes in v2:
time: 88.2 us; the launch traced here: 87.7 us
  starting transfers between devices  43.2 us (49%)
  blocking collectives  29.2 us (33%)
  Pallas kernels  8.59 us (10%)
  local copies, waits for them, and re-layouts  4.07 us (5%)
  waiting for transfers between devices  2.47 us (3%)
    all_to_all x1, blocking collectives, local(): mine = lax.all_to_all(spread, GY, 0, 0, tiled=True)  21.3 us
    ppermute x1, starting transfers between devices, local(): x_inner = lax.ppermute(own, 'xl', swap_inner(2))  13.6 us
    all_to_all x1, blocking collectives, local(): parts = lax.all_to_all(partial_value, ('xl', 'yp'), 0, 0, tiled=True)  7.93 us
    ppermute x1, starting transfers between devices, local(): y_outer = lax.ppermute(own, GY, swap_outer(16))  6.43 us
    ppermute x1, starting transfers between devices, local(): x_outer = lax.ppermute(own, GX, swap_outer(16))  5.75 us
    ppermute x1, starting transfers between devices, local(): z_high = lax.ppermute(own[0:1], 'gz', shift(4, -1))  5.65 us
    ppermute x1, starting transfers between devices, local(): z_low = lax.ppermute(own[7:8], 'gz', shift(4, 1))  5.11 us
    ppermute x1, starting transfers between devices, local(): other = lax.ppermute(mine, 'xl', swap_inner(2))  4.69 us
  transfers between devices with their start and end apart: 7, of which 2 were waited for; matrix products, arithmetic and copies ran while one was open for 1% of the time, Pallas kernels for 3%

profile of v2, /device:TPU:1, one launch (start us, length us, event | category | flops | bytes accessed | tf_op | source)
XLA Modules:
  0.0 87.7 jit_solution(9218029015058350519)
XLA Ops:
  0.0 6.4 %collective-permute-start.3 = (bf16[8,2,32,128]{3,2,1,0:T(8,128)(2,1)}, bf16[8,2,32,128]{3,2,1,0:T(8,128)(2,1)S(1)}, u32[]{:S(2)}, u32[]{:S(2)}) collective-permute-start(bf16[8,2,32,128]{3,2,1,0:T(8,128)(2,1)} %bitcast.13), channel_id=1, source_target_pairs={{0,60},{4,8},{8,4},{12,16},{16,12},{20,24},{24,20},{28,32},{32,28}... | collective-permute-start | bytes 393224 | tf_op jit(solution)/shard_map/ppermute | solution.py:235
  6.4 1.9 %collective-permute-start.2 = (bf16[8,2,32,128]{3,2,1,0:T(8,128)(2,1)}, bf16[8,2,32,128]{3,2,1,0:T(8,128)(2,1)S(1)}, u32[]{:S(2)}, u32[]{:S(2)}) collective-permute-start(bf16[8,2,32,128]{3,2,1,0:T(8,128)(2,1)} %bitcast.14), channel_id=1, source_target_pairs={{0,4},{4,0},{1,5},{5,1},{2,6},{6,2},{3,7},{7,3},{8,12},{12,8},{9,1... | collective-permute-start | bytes 393224 | tf_op jit(solution)/shard_map/ppermute | solution.py:234
  8.4 5.8 %collective-permute-start.1 = (bf16[8,2,32,128]{3,2,1,0:T(8,128)(2,1)}, bf16[8,2,32,128]{3,2,1,0:T(8,128)(2,1)S(1)}, u32[]{:S(2)}, u32[]{:S(2)}) collective-permute-start(bf16[8,2,32,128]{3,2,1,0:T(8,128)(2,1)} %bitcast.15), channel_id=1, source_target_pairs={{0,960},{64,128},{128,64},{192,256},{256,192},{320,384},{384,320},... | collective-permute-start | bytes 393224 | tf_op jit(solution)/shard_map/ppermute | solution.py:233
  14.1 13.6 %collective-permute-start = (bf16[8,2,32,128]{3,2,1,0:T(8,128)(2,1)}, bf16[8,2,32,128]{3,2,1,0:T(8,128)(2,1)S(1)}, u32[]{:S(2)}, u32[]{:S(2)}) collective-permute-start(bf16[8,2,32,128]{3,2,1,0:T(8,128)(2,1)} %bitcast.16), channel_id=1, source_target_pairs={{0,64},{64,0},{1,65},{65,1},{2,66},{66,2},{3,67},{67,3},{4,68},{68... | collective-permute-start | bytes 393224 | tf_op jit(solution)/shard_map/ppermute | solution.py:232
  27.7 0.7 slice_bitcast_fusion
  28.5 5.7 %collective-permute-start.5 = (bf16[1,2,32,128]{3,2,1,0:T(8,128)(2,1)S(1)}, bf16[1,2,32,128]{3,2,1,0:T(8,128)(2,1)S(1)}, u32[]{:S(2)}, u32[]{:S(2)}) collective-permute-start(bf16[1,2,32,128]{3,2,1,0:T(8,128)(2,1)S(1)} %get-tuple-element.11), channel_id=1, source_target_pairs={{0,3},{1,0},{2,1},{3,2},{4,7},{5,4},{6,5},{7,6},{8,11},{9,8},{10,9... | collective-permute-start | bytes 49160 | tf_op jit(solution)/shard_map/ppermute | solution.py:231
  34.1 0.8 collective-permute-done.5.zh_ref
  35.0 5.1 %collective-permute-start.4 = (bf16[1,2,32,128]{3,2,1,0:T(8,128)(2,1)S(1)}, bf16[1,2,32,128]{3,2,1,0:T(8,128)(2,1)S(1)}, u32[]{:S(2)}, u32[]{:S(2)}) collective-permute-start(bf16[1,2,32,128]{3,2,1,0:T(8,128)(2,1)S(1)} %get-tuple-element.12), channel_id=1, source_target_pairs={{0,1},{1,2},{2,3},{3,0},{4,5},{5,6},{6,7},{7,4},{8,9},{9,10},{10,1... | collective-permute-start | bytes 49160 | tf_op jit(solution)/shard_map/ppermute | solution.py:230
  40.1 0.0 copy-start
  40.1 1.7 %copy-done = bf16[1,1,8,2,9,64,128]{6,5,4,3,2,1,0:T(8,128)(2,1)S(1)} copy-done((bf16[1,1,8,2,9,64,128]{6,5,4,3,2,1,0:T(8,128)(2,1)S(1)}, bf16[1,1,8,2,9,64,128]{6,5,4,3,2,1,0:T(8,128)(2,1)}, u32[]{:S(2)}) %copy-start) | copy-done | bytes 2359320
  41.8 0.0 copy-start.1
  41.8 0.9 %copy-done.1 = bf16[1,1,8,2,32,128]{5,4,3,2,1,0:T(8,128)(2,1)S(1)} copy-done((bf16[1,1,8,2,32,128]{5,4,3,2,1,0:T(8,128)(2,1)S(1)}, bf16[1,1,8,2,32,128]{5,4,3,2,1,0:T(8,128)(2,1)}, u32[]{:S(2)}) %copy-start.1) | copy-done | bytes 131096
  42.7 0.0 copy-start.3
  42.7 0.7 copy-done.3
  43.4 2.7 %inside.1 = (bf16[4,4,16,128]{3,2,1,0:T(8,128)(2,1)S(1)}, f32[4,64,64]{2,1,0:T(8,128)S(1)}, bf16[4,64,256]{2,1,0:T(8,128)(2,1)S(1)}) custom-call(s32[4,9]{1,0:T(4,128)S(1)} %bitcast.19, bf16[8,2,9,64,128]{4,3,2,1,0:T(8,128)(2,1)S(1)} %bitcast.11, bf16[8,2,32,128]{3,2,1,0:T(8,128)(2,1)S(1)} %bitcast.17), custom_call_target="tpu_custom_call" | custom-call | flops 150000000 | bytes 3000000 | tf_op jit(solution)/shard_map/inside/pallas_call | solution.py:240
  46.1 0.0 collective-permute-done.4.zl_ref
  46.1 0.0 collective-permute-done.3.yb_ref
  46.1 0.0 collective-permute-done.2.ya_ref
  46.1 0.0 collective-permute-done.1.xb_ref
  46.1 0.0 collective-permute-done.xa_ref
  46.1 0.0 copy-start.2
  46.1 3.3 %across.1 = bf16[4,9,16,128]{3,2,1,0:T(8,128)(2,1)S(1)} custom-call(s32[4,9]{1,0:T(4,128)S(1)} %bitcast.20, bf16[8,2,9,64,128]{4,3,2,1,0:T(8,128)(2,1)S(1)} %bitcast.12, bf16[8,2,32,128]{3,2,1,0:T(8,128)(2,1)S(1)} %collective-permute-done.xa_ref, bf16[8,2,32,128]{3,2,1,0:T(8,128)(2,1)S(1)} %collective-permute-done.1.xb_ref, ...), custom_call_target="tpu_custom_call" | custom-call | flops 150000000 | bytes 3000000 | tf_op jit(solution)/shard_map/across/pallas_call | solution.py:254
  49.5 7.9 %all_to_all.10 = bf16[4,9,16,128]{3,2,1,0:T(8,128)(2,1)S(1)} all-to-all(bf16[4,9,16,128]{3,2,1,0:T(8,128)(2,1)S(1)} %across.1), channel_id=1, replica_groups=mesh['xh'=8,'xl'=2,'yl'=2,'yh'=4,'yp'=2,'gz'=4] {'xl','yp'}, dimensions={0} | all-to-all | bytes 294912 | tf_op jit(solution)/shard_map/all_to_all | solution.py:263
  57.4 0.1 broadcast_in_dim.4
  57.5 21.3 %all_to_all.11.own_ref = bf16[16,9,16,128]{3,2,1,0:T(8,128)(2,1)S(1)} all-to-all(bf16[16,9,16,128]{3,2,1,0:T(8,128)(2,1)S(1)} %broadcast_in_dim.4), channel_id=1, replica_groups=mesh['xh'=8,'xl'=2,'yl'=2,'yh'=4,'yp'=2,'gz'=4] {'yl','yh','yp'}, dimensions={0} | all-to-all | bytes 1179648 | tf_op jit(solution)/shard_map/all_to_all | solution.py:266
  78.8 4.7 %collective-permute-start.6 = (bf16[16,9,16,128]{3,2,1,0:T(8,128)(2,1)S(1)}, bf16[16,9,16,128]{3,2,1,0:T(8,128)(2,1)S(1)}, u32[]{:S(2)}, u32[]{:S(2)}) collective-permute-start(bf16[16,9,16,128]{3,2,1,0:T(8,128)(2,1)S(1)} %all_to_all.11.own_ref), channel_id=1, source_target_pairs={{0,64},{64,0},{1,65},{65,1},{2,66},{66,2},{3,67},{67,3},{4,68},{68... | collective-permute-start | bytes 1769480 | tf_op jit(solution)/shard_map/ppermute | solution.py:267
  83.5 1.6 %collective-permute-done.6.other_ref = bf16[16,9,16,128]{3,2,1,0:T(8,128)(2,1)S(1)} collective-permute-done((bf16[16,9,16,128]{3,2,1,0:T(8,128)(2,1)S(1)}, bf16[16,9,16,128]{3,2,1,0:T(8,128)(2,1)S(1)}, u32[]{:S(2)}, u32[]{:S(2)}) %collective-permute-start.6) | collective-permute-done | bytes 589856 | tf_op jit(solution)/shard_map/ppermute | solution.py:267
  85.1 0.0 copy-done.2
  85.1 2.5 %place.1 = f32[9,16,2048]{2,1,0:T(8,128)} custom-call(s32[8,8,16]{2,1,0:T(8,128)S(1)} %bitcast.18, bf16[16,9,16,128]{3,2,1,0:T(8,128)(2,1)S(1)} %all_to_all.11.own_ref, bf16[16,9,16,128]{3,2,1,0:T(8,128)(2,1)S(1)} %collective-permute-done.6.other_ref), custom_call_target="tpu_custom_call" | custom-call | tf_op jit(solution)/shard_map/place/pallas_call | solution.py:268
  (1 shorter events, 0.0 us)
Async XLA Ops:
  0.0 46.1 %collective-permute-start.3 = (bf16[8,2,32,128]{3,2,1,0:T(8,128)(2,1)}, bf16[8,2,32,128]{3,2,1,0:T(8,128)(2,1)S(1)}, u32[]{:S(2)}, u32[]{:S(2)}) collective-permute-start(bf16[8,2,32,128]{3,2,1,0:T(8,128)(2,1)} %bitcast.13), channel_id=1, source_target_pairs={{0,60},{4,8},{8,4},{12,16},{16,12},{20,24},{24,20},{28,32},{32,28}... | collective-permute-start | bytes 393224 | tf_op jit(solution)/shard_map/ppermute | solution.py:235
  6.4 39.7 %collective-permute-start.2 = (bf16[8,2,32,128]{3,2,1,0:T(8,128)(2,1)}, bf16[8,2,32,128]{3,2,1,0:T(8,128)(2,1)S(1)}, u32[]{:S(2)}, u32[]{:S(2)}) collective-permute-start(bf16[8,2,32,128]{3,2,1,0:T(8,128)(2,1)} %bitcast.14), channel_id=1, source_target_pairs={{0,4},{4,0},{1,5},{5,1},{2,6},{6,2},{3,7},{7,3},{8,12},{12,8},{9,1... | collective-permute-start | bytes 393224 | tf_op jit(solution)/shard_map/ppermute | solution.py:234
  8.4 37.7 %collective-permute-start.1 = (bf16[8,2,32,128]{3,2,1,0:T(8,128)(2,1)}, bf16[8,2,32,128]{3,2,1,0:T(8,128)(2,1)S(1)}, u32[]{:S(2)}, u32[]{:S(2)}) collective-permute-start(bf16[8,2,32,128]{3,2,1,0:T(8,128)(2,1)} %bitcast.15), channel_id=1, source_target_pairs={{0,960},{64,128},{128,64},{192,256},{256,192},{320,384},{384,320},... | collective-permute-start | bytes 393224 | tf_op jit(solution)/shard_map/ppermute | solution.py:233
  14.1 32.0 %collective-permute-start = (bf16[8,2,32,128]{3,2,1,0:T(8,128)(2,1)}, bf16[8,2,32,128]{3,2,1,0:T(8,128)(2,1)S(1)}, u32[]{:S(2)}, u32[]{:S(2)}) collective-permute-start(bf16[8,2,32,128]{3,2,1,0:T(8,128)(2,1)} %bitcast.16), channel_id=1, source_target_pairs={{0,64},{64,0},{1,65},{65,1},{2,66},{66,2},{3,67},{67,3},{4,68},{68... | collective-permute-start | bytes 393224 | tf_op jit(solution)/shard_map/ppermute | solution.py:232
  28.5 6.5 %collective-permute-start.5 = (bf16[1,2,32,128]{3,2,1,0:T(8,128)(2,1)S(1)}, bf16[1,2,32,128]{3,2,1,0:T(8,128)(2,1)S(1)}, u32[]{:S(2)}, u32[]{:S(2)}) collective-permute-start(bf16[1,2,32,128]{3,2,1,0:T(8,128)(2,1)S(1)} %get-tuple-element.11), channel_id=1, source_target_pairs={{0,3},{1,0},{2,1},{3,2},{4,7},{5,4},{6,5},{7,6},{8,11},{9,8},{10,9... | collective-permute-start | bytes 49160 | tf_op jit(solution)/shard_map/ppermute | solution.py:231
  35.0 11.1 %collective-permute-start.4 = (bf16[1,2,32,128]{3,2,1,0:T(8,128)(2,1)S(1)}, bf16[1,2,32,128]{3,2,1,0:T(8,128)(2,1)S(1)}, u32[]{:S(2)}, u32[]{:S(2)}) collective-permute-start(bf16[1,2,32,128]{3,2,1,0:T(8,128)(2,1)S(1)} %get-tuple-element.12), channel_id=1, source_target_pairs={{0,1},{1,2},{2,3},{3,0},{4,5},{5,6},{6,7},{7,4},{8,9},{9,10},{10,1... | collective-permute-start | bytes 49160 | tf_op jit(solution)/shard_map/ppermute | solution.py:230
  40.1 1.7 %copy-start = (bf16[1,1,8,2,9,64,128]{6,5,4,3,2,1,0:T(8,128)(2,1)S(1)}, bf16[1,1,8,2,9,64,128]{6,5,4,3,2,1,0:T(8,128)(2,1)}, u32[]{:S(2)}) copy-start(bf16[1,1,8,2,9,64,128]{6,5,4,3,2,1,0:T(8,128)(2,1)} %param.4) | copy-start | bytes 7077892
  41.8 0.9 %copy-start.1 = (bf16[1,1,8,2,32,128]{5,4,3,2,1,0:T(8,128)(2,1)S(1)}, bf16[1,1,8,2,32,128]{5,4,3,2,1,0:T(8,128)(2,1)}, u32[]{:S(2)}) copy-start(bf16[1,1,8,2,32,128]{5,4,3,2,1,0:T(8,128)(2,1)} %param.5) | copy-start | bytes 393220
  42.7 0.7 copy-start.3
  46.1 39.0 %copy-start.2 = (s32[8,8,16,1]{2,3,1,0:T(1,128)S(1)}, s32[8,8,16,1]{2,3,1,0:T(1,128)}, u32[]{:S(2)}) copy-start(s32[8,8,16,1]{2,3,1,0:T(1,128)} %param.7) | copy-start | bytes 12292
  78.8 6.3 %collective-permute-start.6 = (bf16[16,9,16,128]{3,2,1,0:T(8,128)(2,1)S(1)}, bf16[16,9,16,128]{3,2,1,0:T(8,128)(2,1)S(1)}, u32[]{:S(2)}, u32[]{:S(2)}) collective-permute-start(bf16[16,9,16,128]{3,2,1,0:T(8,128)(2,1)S(1)} %all_to_all.11.own_ref), channel_id=1, source_target_pairs={{0,64},{64,0},{1,65},{65,1},{2,66},{66,2},{3,67},{67,3},{4,68},{68... | collective-permute-start | bytes 1769480 | tf_op jit(solution)/shard_map/ppermute | solution.py:267

commit v3 on v2

v3 whole, which is shorter than its diff:
```python
import jax
import jax.numpy as jnp
from jax import lax
from jax.experimental import pallas as pl
from jax.experimental.pallas import tpu as pltpu
from jax.sharding import Mesh, PartitionSpec as P

F32 = jnp.float32
BF16 = jnp.bfloat16
GX = ("xh", "xl")
GY = ("yl", "yh", "yp")


def swap_inner(count):
    return [(i, i ^ 1) for i in range(count)]


def shift(count, step):
    return [(i, (i + step) % count) for i in range(count)]


def lane_index(shape):
    return lax.broadcasted_iota(jnp.int32, shape, 1)


def block_of(vectors, signs):
    return jnp.concatenate(
        [vectors * signs, jnp.concatenate([vectors[:, 64:], vectors[:, :64]], 1)], 0
    )


def lane_signs():
    return jnp.where(lane_index((32, 128)) < 64, 1.0, -1.0).astype(BF16)


def hop(link_block, rows):
    out = lax.dot_general(link_block, rows, (((1,), (1,)), ((), ())), preferred_element_type=F32)
    return out.astype(BF16)


def project(own, stacked):
    return jnp.dot(own, stacked, preferred_element_type=F32)


def fold(result):
    first = jnp.concatenate([result[0:16], result[16:32]], 1)
    second = jnp.concatenate([result[32:48], result[48:64]], 1)
    low = lane_index((16, 128)) % 64 < 32
    return first + jnp.where(low, pltpu.roll(second, 96, 1), -pltpu.roll(second, 32, 1))


def roles_of(role_ref):
    return role_ref[8], [role_ref[axis] for axis in range(4)], [role_ref[4 + axis] for axis in range(4)]


def prepare_kernel(
    off_ref, v_ref, role_ref, low_ref, high_ref, rows_ref, own_ref, first_ref, second_ref, vf_ref
):
    k_self = jnp.int32(36)
    for place, (axis, sign) in enumerate([(a, g) for g in (-1, 1) for a in range(4)]):
        index = jnp.int32(0)
        for k in range(9):
            index = index + jnp.where(off_ref[axis, k] == sign, k, 0).astype(jnp.int32)
        role_ref[place] = index
        k_self = k_self - index
    role_ref[8] = k_self
    low_ref[0] = v_ref[0]
    high_ref[0] = v_ref[7]
    signs = lane_signs()
    for z in range(8):
        for t in range(2):
            vf_ref[pl.ds((2 * z + t) * 32, 32), :] = v_ref[z, t].astype(F32)
            rows_ref[2 * z + t] = block_of(v_ref[z, t], signs)
    low = lane_index((16, 128)) < 64
    low_own = lane_index((64, 128)) < 64
    for z in range(8):
        base = z * 64
        quarter = []
        for first in range(2):
            left = vf_ref[pl.ds(base + first, 16, stride=2), :]
            right = vf_ref[pl.ds(base + 32 + first, 16, stride=2), :]
            quarter.append(
                (
                    jnp.where(low, left, pltpu.roll(right, 64, 1)),
                    jnp.where(low, pltpu.roll(left, 64, 1), right),
                )
            )
        half = jnp.concatenate([quarter[0][0], quarter[1][0], quarter[0][1], quarter[1][1]], 0)
        lanes = slice((z % 2) * 128, (z % 2) * 128 + 128)
        own_ref[z // 2, :, lanes] = half.astype(BF16)
        first_ref[z // 2, :, lanes] = jnp.where(low_own, half, 0.0).astype(BF16)
        second_ref[z // 2, :, lanes] = jnp.where(low_own, 0.0, half).astype(BF16)


def inside_kernel(
    off_ref, links_ref, rows_ref, own_ref, first_ref, second_ref, part_ref, acc_ref, hop_ref
):
    k_self, minus, plus = roles_of(off_ref)
    for z in range(8):
        agg = z // 2
        for t in range(2):
            k_tin = plus[3] if t == 1 else minus[3]
            k_tout = minus[3] if t == 1 else plus[3]
            k_zin = minus[2] if z % 2 == 0 else plus[2]
            target = z - 1 if z % 2 == 0 else z + 1
            stack = [
                links_ref[z, t, k_self],
                links_ref[z, 1 - t, k_tin],
                links_ref[z ^ 1, t, k_zin],
                links_ref[z, 1 - t, k_tout],
            ]
            if 0 <= target <= 7:
                k_back = plus[2] if z % 2 == 0 else minus[2]
                stack.append(links_ref[target, t, k_back])
            res = hop(jnp.concatenate(stack, 0), rows_ref[2 * z + t])
            here = (2 * (z % 2) + t) * 64
            side = (2 * (z % 2) + 1 - t) * 64
            across = (2 * (1 - z % 2) + t) * 64
            hop_ref[agg, here : here + 64] = res[0:64]
            hop_ref[agg, 256 + side : 256 + side + 64] = res[64:128]
            hop_ref[agg, 512 + across : 512 + across + 64] = res[128:192]
            hop_ref[agg, 768 + side : 768 + side + 64] = res[192:256]
            if 0 <= target <= 7:
                row = 1024 + (2 * (target % 2) + t) * 64
                hop_ref[target // 2, row : row + 64] = res[256:320]
    for agg in range(4):
        own = own_ref[agg]
        acc_ref[agg] = project(jnp.concatenate([own] * 3, 1), hop_ref[agg, 0:768])
        part_ref[agg, 0] = fold(project(first_ref[agg], hop_ref[agg, 768:1024])).astype(BF16)
        part_ref[agg, 1] = fold(project(second_ref[agg], hop_ref[agg, 768:1024])).astype(BF16)
        if agg > 0:
            part_ref[agg, 2] = fold(project(own[:, :128], hop_ref[agg, 1024:1152])).astype(BF16)
        if agg < 3:
            part_ref[agg, 3] = fold(project(own[:, 128:], hop_ref[agg, 1152:1280])).astype(BF16)
    part_ref[0, 2] = jnp.zeros((16, 128), BF16)
    part_ref[3, 3] = jnp.zeros((16, 128), BF16)


def across_kernel(
    role_ref,
    links_ref,
    xl_ref,
    xh_ref,
    yl_ref,
    yh_ref,
    zl_ref,
    zh_ref,
    part_ref,
    acc_ref,
    own_ref,
    out_ref,
    rows_ref,
    hop_ref,
):
    k_self, minus, plus = roles_of(role_ref)
    x_odd = lax.axis_index("xl")
    y_odd = lax.axis_index("yp")
    x_out = jnp.where(x_odd == 1, plus[0], minus[0])
    x_in = jnp.where(x_odd == 1, minus[0], plus[0])
    y_out = jnp.where(y_odd == 1, plus[1], minus[1])
    y_in = jnp.where(y_odd == 1, minus[1], plus[1])
    x_base = pl.multiple_of(512 * x_odd, 256)
    y_base = pl.multiple_of(512 * y_odd, 256)
    zero = jnp.zeros((16, 128), BF16)
    signs = lane_signs()
    sides = (
        (xl_ref, minus[0], 512 - x_base),
        (xh_ref, plus[0], x_base),
        (yl_ref, minus[1], 768 - y_base),
        (yh_ref, plus[1], 256 + y_base),
    )
    for t in range(2):
        rows_ref[64 + t] = block_of(zl_ref[0, t], signs)
        rows_ref[66 + t] = block_of(zh_ref[0, t], signs)
    for z in range(8):
        for t in range(2):
            for role, (ref, _, _) in enumerate(sides):
                rows_ref[role * 16 + 2 * z + t] = block_of(ref[z, t], signs)
    for t in range(2):
        hop_ref[0, 1024 + t * 64 : 1088 + t * 64] = hop(links_ref[0, t, minus[2]], rows_ref[64 + t])
        hop_ref[3, 1024 + t * 64 : 1088 + t * 64] = hop(links_ref[7, t, plus[2]], rows_ref[66 + t])
    for z in range(8):
        for t in range(2):
            for role, (_, k, base) in enumerate(sides):
                row = pl.multiple_of(base + (2 * (z % 2) + t) * 64, 64)
                res = hop(links_ref[z, t, k], rows_ref[role * 16 + 2 * z + t])
                hop_ref[z // 2, pl.ds(row, 64)] = res
    for agg in range(4):
        own = own_ref[agg]
        total = acc_ref[agg] + project(jnp.concatenate([own] * 2, 1), hop_ref[agg, 0:512])
        out_ref[agg, k_self] = fold(total).astype(BF16)
        out_ref[agg, x_out] = fold(project(own, hop_ref[agg, 512:768])).astype(BF16)
        out_ref[agg, y_out] = fold(project(own, hop_ref[agg, 768:1024])).astype(BF16)
        out_ref[agg, x_in] = zero
        out_ref[agg, y_in] = zero
        out_ref[agg, minus[3]] = part_ref[agg, 0]
        out_ref[agg, plus[3]] = part_ref[agg, 1]
        if agg > 0:
            out_ref[agg, minus[2]] = part_ref[agg, 2]
        else:
            out_ref[agg, minus[2]] = fold(project(own[:, :128], hop_ref[0, 1024:1152])).astype(BF16)
        if agg < 3:
            out_ref[agg, plus[2]] = part_ref[agg, 3]
        else:
            out_ref[agg, plus[2]] = fold(project(own[:, 128:], hop_ref[3, 1024:1152])).astype(BF16)


def place_kernel(place_ref, own_ref, other_ref, out_ref, table_ref, wide_ref, buf_ref, sems):
    line = lax.axis_index("xh")
    column = lax.axis_index("xl")
    block = lax.axis_index("gz")

    for entry in range(32):
        target = place_ref[line, entry // 4, block * 4 + entry % 4]
        table_ref[target] = jnp.int32(entry)

    def gather(slot, carry):
        entry = table_ref[column * 16 + slot]
        source = 2 * (entry // 4) + entry % 2
        is_own = (entry % 4) // 2 == column
        rows = pl.ds(pl.multiple_of(slot * 16, 16), 16)
        for k in range(9):
            picked = jnp.where(is_own, own_ref[source, k].astype(F32), other_ref[source, k].astype(F32))
            wide_ref[k, rows, :] = picked
        return carry

    lax.fori_loop(0, 16, gather, 0, unroll=4)
    copies = []
    for k in range(9):
        for lane in range(16):
            buf_ref[k, :, lane * 128 : (lane + 1) * 128] = wide_ref[k, pl.ds(lane, 16, stride=16), :]
        copies.append(pltpu.make_async_copy(buf_ref.at[k], out_ref.at[k], sems.at[k]))
        copies[k].start()
    for copy in copies:
        copy.wait()


def local(links, null_vectors, offsets, place):
    own = null_vectors[0, 0]
    links = links[0, 0]
    vmem = pl.BlockSpec(memory_space=pltpu.VMEM)
    smem = pl.BlockSpec(memory_space=pltpu.SMEM)
    anywhere = pl.BlockSpec(memory_space=pl.ANY)
    role_table, slab_low, slab_high, rows, packed, packed_first, packed_second = pl.pallas_call(
        prepare_kernel,
        out_shape=(jax.ShapeDtypeStruct((9,), jnp.int32),)
        + (jax.ShapeDtypeStruct((1, 2, 32, 128), BF16),) * 2
        + (jax.ShapeDtypeStruct((16, 64, 128), BF16),)
        + (jax.ShapeDtypeStruct((4, 64, 256), BF16),) * 3,
        in_specs=[smem, vmem],
        out_specs=(smem,) + (vmem,) * 6,
        scratch_shapes=[pltpu.VMEM((512, 128), F32)],
        compiler_params=pltpu.CompilerParams(vmem_limit_bytes=16 * 1024 * 1024),
        cost_estimate=pl.CostEstimate(
            flops=2_000_000_000, bytes_accessed=10_000_000, transcendentals=0
        ),
        name="prepare",
    )(offsets.T, own)
    z_low = lax.ppermute(slab_high, "gz", shift(4, 1))
    z_high = lax.ppermute(slab_low, "gz", shift(4, -1))
    y_low = lax.ppermute(own, GY, shift(16, 1))
    y_high = lax.ppermute(own, GY, shift(16, -1))
    x_low = lax.ppermute(own, GX, shift(16, 1))
    x_high = lax.ppermute(own, GX, shift(16, -1))
    part, acc = pl.pallas_call(
        inside_kernel,
        out_shape=(
            jax.ShapeDtypeStruct((4, 4, 16, 128), BF16),
            jax.ShapeDtypeStruct((4, 64, 64), F32),
        ),
        in_specs=[smem] + [vmem] * 5,
        out_specs=(vmem, vmem),
        scratch_shapes=[pltpu.VMEM((4, 1280, 64), BF16)],
        compiler_params=pltpu.CompilerParams(vmem_limit_bytes=16 * 1024 * 1024),
        cost_estimate=pl.CostEstimate(flops=150_000_000, bytes_accessed=3_000_000, transcendentals=0),
        name="inside",
    )(role_table, links, rows, packed, packed_first, packed_second)
    partial_value = pl.pallas_call(
        across_kernel,
        out_shape=jax.ShapeDtypeStruct((4, 9, 16, 128), BF16),
        in_specs=[smem] + [vmem] * 10,
        out_specs=vmem,
        scratch_shapes=[pltpu.VMEM((68, 64, 128), BF16), pltpu.VMEM((4, 1152, 64), BF16)],
        compiler_params=pltpu.CompilerParams(vmem_limit_bytes=16 * 1024 * 1024),
        cost_estimate=pl.CostEstimate(flops=150_000_000, bytes_accessed=3_000_000, transcendentals=0),
        name="across",
    )(role_table, links, x_low, x_high, y_low, y_high, z_low, z_high, part, acc, packed)
    parts = lax.all_to_all(partial_value, ("xl", "yp"), 0, 0, tiled=True)
    chunk = jnp.sum(parts.astype(F32), axis=0).astype(BF16)
    spread = jnp.broadcast_to(chunk[None], (16, 9, 16, 128))
    mine = lax.all_to_all(spread, GY, 0, 0, tiled=True)
    other = lax.ppermute(mine, "xl", swap_inner(2))
    placed = pl.pallas_call(
        place_kernel,
        out_shape=jax.ShapeDtypeStruct((9, 16, 2048), F32),
        in_specs=[smem, vmem, vmem],
        out_specs=anywhere,
        scratch_shapes=[
            pltpu.SMEM((32,), jnp.int32),
            pltpu.VMEM((9, 256, 128), F32),
            pltpu.VMEM((9, 16, 2048), F32),
            pltpu.SemaphoreType.DMA((9,)),
        ],
        compiler_params=pltpu.CompilerParams(vmem_limit_bytes=32 * 1024 * 1024),
        name="place",
    )(place.reshape(8, 8, 16), mine, other)
    return jnp.transpose(placed, (1, 0, 2))[None, None]


def solution(mesh):
    fine = Mesh(mesh.devices.reshape(8, 2, 2, 4, 2, 4), ("xh", "xl", "yl", "yh", "yp", "gz"))
    placed = (P(GX, GY, "gz"), P(GX, GY, "gz"), P(), P())
    return jax.shard_map(
        local,
        mesh=fine,
        in_specs=placed,
        out_specs=P(GX, "gz"),
        check_vma=False,
    )
```

time: 88.2 us -> 81.5 us (0.924)
  starting transfers between devices: 43.2 us -> 28.5 us
  blocking collectives: 29.2 us -> 35.4 us
  waiting for transfers between devices: 2.47 us -> 8.33 us
  local copies, waits for them, and re-layouts: 4.07 us -> 1.71 us
  Pallas kernels: 8.59 us -> 7.13 us
    ppermute x6, starting transfers between devices: 38.5 us -> 23.8 us  [the longest x1 11.6 us: local(): x_high = lax.ppermute(own, GX, shift(16, -1))]
    ppermute x6, waiting for transfers between devices: 0.86 us -> 6.72 us  [the longest x1 4.66 us: local(): z_low = lax.ppermute(slab_high, 'gz', shift(4, 1))]
    all_to_all x1, blocking collectives: 7.93 us -> 12.9 us  [local(): parts = lax.all_to_all(partial_value, ('xl', 'yp'), 0, 0, tiled=True)]
    unnamed x8, local copies, waits for them, and re-layouts: 3.25 us -> 1.63 us
    pallas_call x1, Pallas kernels: 3.32 us -> 1.85 us  [local(): pl.pallas_call(across_kernel, out_shape=jax.ShapeDtypeStruct((4, 9, 16, 1...]
    pallas_call x0 -> x1, Pallas kernels: none -> 1.34 us  [local(): pl.pallas_call(prepare_kernel, out_shape=(jax.ShapeDtypeStruct((9,), jnp....]
    pallas_call x1, Pallas kernels: 2.74 us -> 1.4 us  [local(): pl.pallas_call(inside_kernel, out_shape=(jax.ShapeDtypeStruct((4, 4, 16,...]
    all_to_all x1, blocking collectives: 21.3 us -> 22.5 us  [local(): mine = lax.all_to_all(spread, GY, 0, 0, tiled=True)]
  transfers between devices with their start and end apart: 7 -> 7, of which waited for: 2 -> 3; matrix products, arithmetic and copies ran while one was open for 1% -> 0% of each run, Pallas kernels for 3% -> 3%
where the time goes in v3:
time: 81.5 us; the launch traced here: 81.1 us
  blocking collectives  35.4 us (43%)
  starting transfers between devices  28.5 us (35%)
  waiting for transfers between devices  8.33 us (10%)
  Pallas kernels  7.13 us (9%)
  local copies, waits for them, and re-layouts  1.71 us (2%)
    all_to_all x1, blocking collectives, local(): mine = lax.all_to_all(spread, GY, 0, 0, tiled=True)  22.5 us
    all_to_all x1, blocking collectives, local(): parts = lax.all_to_all(partial_value, ('xl', 'yp'), 0, 0, tiled=True)  12.9 us
    ppermute x1, starting transfers between devices, local(): x_high = lax.ppermute(own, GX, shift(16, -1))  11.6 us
    ppermute x1, starting transfers between devices, local(): y_high = lax.ppermute(own, GY, shift(16, -1))  6.43 us
    ppermute x1, starting transfers between devices, local(): other = lax.ppermute(mine, 'xl', swap_inner(2))  4.69 us
    ppermute x1, waiting for transfers between devices, local(): z_low = lax.ppermute(slab_high, 'gz', shift(4, 1))  4.66 us
    pallas_call x1, Pallas kernels, local(): pl.pallas_call(place_kernel, out_shape=jax.ShapeDtypeStruct((9, 16, 2048)...  2.54 us
    ppermute x1, waiting for transfers between devices, local(): z_high = lax.ppermute(slab_low, 'gz', shift(4, -1))  2.05 us
  transfers between devices with their start and end apart: 7, of which 3 were waited for; matrix products, arithmetic and copies ran while one was open for 0% of the time, Pallas kernels for 3%

profile of v3, /device:TPU:1, one launch (start us, length us, event | category | flops | bytes accessed | tf_op | source)
XLA Modules:
  0.0 81.1 jit_solution(6886819823356129886)
XLA Ops:
  0.0 6.4 %collective-permute-start.3 = (bf16[8,2,32,128]{3,2,1,0:T(8,128)(2,1)}, bf16[8,2,32,128]{3,2,1,0:T(8,128)(2,1)S(1)}, u32[]{:S(2)}, u32[]{:S(2)}) collective-permute-start(bf16[8,2,32,128]{3,2,1,0:T(8,128)(2,1)} %bitcast.10), channel_id=1, source_target_pairs={{0,60},{4,0},{8,4},{12,8},{16,12},{20,16},{24,20},{28,24},{32,28},... | collective-permute-start | bytes 393224 | tf_op jit(solution)/shard_map/ppermute | solution.py:262
  6.4 1.9 %collective-permute-start.2 = (bf16[8,2,32,128]{3,2,1,0:T(8,128)(2,1)}, bf16[8,2,32,128]{3,2,1,0:T(8,128)(2,1)S(1)}, u32[]{:S(2)}, u32[]{:S(2)}) collective-permute-start(bf16[8,2,32,128]{3,2,1,0:T(8,128)(2,1)} %bitcast.11), channel_id=1, source_target_pairs={{0,4},{4,8},{8,12},{12,16},{16,20},{20,24},{24,28},{28,32},{32,36}... | collective-permute-start | bytes 393224 | tf_op jit(solution)/shard_map/ppermute | solution.py:261
  8.4 11.6 %collective-permute-start.1 = (bf16[8,2,32,128]{3,2,1,0:T(8,128)(2,1)}, bf16[8,2,32,128]{3,2,1,0:T(8,128)(2,1)S(1)}, u32[]{:S(2)}, u32[]{:S(2)}) collective-permute-start(bf16[8,2,32,128]{3,2,1,0:T(8,128)(2,1)} %bitcast.12), channel_id=1, source_target_pairs={{0,960},{64,0},{128,64},{192,128},{256,192},{320,256},{384,320},{4... | collective-permute-start | bytes 393224 | tf_op jit(solution)/shard_map/ppermute | solution.py:264
  20.0 0.0 collective-permute-start
  20.0 0.0 copy-start.2
  20.0 0.9 %copy-done.2 = bf16[1,1,8,2,32,128]{5,4,3,2,1,0:T(8,128)(2,1)S(1)} copy-done((bf16[1,1,8,2,32,128]{5,4,3,2,1,0:T(8,128)(2,1)S(1)}, bf16[1,1,8,2,32,128]{5,4,3,2,1,0:T(8,128)(2,1)}, u32[]{:S(2)}) %copy-start.2) | copy-done | bytes 131096
  20.9 0.0 copy-start.3
  20.9 0.7 copy-done.3
  21.6 0.0 copy-start
  21.6 1.3 %prepare.1 = (s32[9]{0:T(128)S(1)}, bf16[1,2,32,128]{3,2,1,0:T(8,128)(2,1)S(1)}, bf16[1,2,32,128]{3,2,1,0:T(8,128)(2,1)S(1)}, bf16[16,64,128]{2,1,0:T(8,128)(2,1...) custom-call(s32[4,9]{1,0:T(4,128)S(1)} %bitcast.15, ...), custom_call_target="tpu_custom_call" | custom-call | flops 2000000000 | bytes 10000000 | tf_op jit(solution)/shard_map/prepare/pallas_call | solution.py:244
  22.9 1.9 %collective-permute-start.4 = (bf16[1,2,32,128]{3,2,1,0:T(8,128)(2,1)S(1)}, bf16[1,2,32,128]{3,2,1,0:T(8,128)(2,1)S(1)}, u32[]{:S(2)}, u32[]{:S(2)}) collective-permute-start(bf16[1,2,32,128]{3,2,1,0:T(8,128)(2,1)S(1)} %get-tuple-element.15), channel_id=1, source_target_pairs={{0,1},{1,2},{2,3},{3,0},{4,5},{5,6},{6,7},{7,4},{8,9},{9,10},{10,1... | collective-permute-start | bytes 49160 | tf_op jit(solution)/shard_map/ppermute | solution.py:259
  24.9 4.7 %collective-permute-done.4.zl_ref = bf16[1,2,32,128]{3,2,1,0:T(8,128)(2,1)S(1)} collective-permute-done((bf16[1,2,32,128]{3,2,1,0:T(8,128)(2,1)S(1)}, bf16[1,2,32,128]{3,2,1,0:T(8,128)(2,1)S(1)}, u32[]{:S(2)}, u32[]{:S(2)}) %collective-permute-start.4) | collective-permute-done | bytes 16416 | tf_op jit(solution)/shard_map/ppermute | solution.py:259
  29.5 1.9 %collective-permute-start.5 = (bf16[1,2,32,128]{3,2,1,0:T(8,128)(2,1)S(1)}, bf16[1,2,32,128]{3,2,1,0:T(8,128)(2,1)S(1)}, u32[]{:S(2)}, u32[]{:S(2)}) collective-permute-start(bf16[1,2,32,128]{3,2,1,0:T(8,128)(2,1)S(1)} %get-tuple-element.16), channel_id=1, source_target_pairs={{0,3},{1,0},{2,1},{3,2},{4,7},{5,4},{6,5},{7,6},{8,11},{9,8},{10,9... | collective-permute-start | bytes 49160 | tf_op jit(solution)/shard_map/ppermute | solution.py:260
  31.5 0.0 copy-done
  31.5 1.4 %inside.1 = (bf16[4,4,16,128]{3,2,1,0:T(8,128)(2,1)S(1)}, f32[4,64,64]{2,1,0:T(8,128)S(1)}) custom-call(s32[9]{0:T(128)S(1)} %get-tuple-element.14.off_ref.role_ref, bf16[8,2,9,64,128]{4,3,2,1,0:T(8,128)(2,1)S(1)} %bitcast.7, bf16[16,64,128]{2,1,0:T(8,128)(2,1)S(1)} %get-tuple-element.17.rows_ref, bf16[4,64,256]{2,1,0:T(8,128)(2,1)S(1)} %get-tuple-element.18.own_ref, ...), custom_call_target="tpu_custom_call" | custom-call | flops 150000000 | bytes 3000000 | tf_op jit(solution)/shard_map/inside/pallas_call | solution.py:265
  32.9 2.0 %collective-permute-done.5.zh_ref = bf16[1,2,32,128]{3,2,1,0:T(8,128)(2,1)S(1)} collective-permute-done((bf16[1,2,32,128]{3,2,1,0:T(8,128)(2,1)S(1)}, bf16[1,2,32,128]{3,2,1,0:T(8,128)(2,1)S(1)}, u32[]{:S(2)}, u32[]{:S(2)}) %collective-permute-start.5) | collective-permute-done | bytes 16416 | tf_op jit(solution)/shard_map/ppermute | solution.py:260
  34.9 0.0 collective-permute-done.3.yh_ref
  34.9 0.0 collective-permute-done.2.yl_ref
  34.9 0.0 collective-permute-done.1.xh_ref
  34.9 0.0 collective-permute-done.xl_ref
  34.9 0.0 copy-start.1
  34.9 1.9 %across.1 = bf16[4,9,16,128]{3,2,1,0:T(8,128)(2,1)S(1)} custom-call(s32[9]{0:T(128)S(1)} %get-tuple-element.14.off_ref.role_ref, bf16[8,2,9,64,128]{4,3,2,1,0:T(8,128)(2,1)S(1)} %bitcast.8, bf16[8,2,32,128]{3,2,1,0:T(8,128)(2,1)S(1)} %collective-permute-done.xl_ref, bf16[8,2,32,128]{3,2,1,0:T(8,128)(2,1)S(1)} %collective-permute-done.1.xh_ref, ...), custom_call_target="tpu_custom_call" | custom-call | flops 150000000 | bytes 3000000 | tf_op jit(solution)/shard_map/across/pallas_call | solution.py:278
  36.8 12.9 %all_to_all.10 = bf16[4,9,16,128]{3,2,1,0:T(8,128)(2,1)S(1)} all-to-all(bf16[4,9,16,128]{3,2,1,0:T(8,128)(2,1)S(1)} %across.1), channel_id=1, replica_groups=mesh['xh'=8,'xl'=2,'yl'=2,'yh'=4,'yp'=2,'gz'=4] {'xl','yp'}, dimensions={0} | all-to-all | bytes 294912 | tf_op jit(solution)/shard_map/all_to_all | solution.py:288
  49.7 0.1 broadcast_in_dim.4
  49.8 22.5 %all_to_all.11.own_ref = bf16[16,9,16,128]{3,2,1,0:T(8,128)(2,1)S(1)} all-to-all(bf16[16,9,16,128]{3,2,1,0:T(8,128)(2,1)S(1)} %broadcast_in_dim.4), channel_id=1, replica_groups=mesh['xh'=8,'xl'=2,'yl'=2,'yh'=4,'yp'=2,'gz'=4] {'yl','yh','yp'}, dimensions={0} | all-to-all | bytes 1179648 | tf_op jit(solution)/shard_map/all_to_all | solution.py:291
  72.3 4.7 %collective-permute-start.6 = (bf16[16,9,16,128]{3,2,1,0:T(8,128)(2,1)S(1)}, bf16[16,9,16,128]{3,2,1,0:T(8,128)(2,1)S(1)}, u32[]{:S(2)}, u32[]{:S(2)}) collective-permute-start(bf16[16,9,16,128]{3,2,1,0:T(8,128)(2,1)S(1)} %all_to_all.11.own_ref), channel_id=1, source_target_pairs={{0,64},{64,0},{1,65},{65,1},{2,66},{66,2},{3,67},{67,3},{4,68},{68... | collective-permute-start | bytes 1769480 | tf_op jit(solution)/shard_map/ppermute | solution.py:292
  77.0 1.6 %collective-permute-done.6.other_ref = bf16[16,9,16,128]{3,2,1,0:T(8,128)(2,1)S(1)} collective-permute-done((bf16[16,9,16,128]{3,2,1,0:T(8,128)(2,1)S(1)}, bf16[16,9,16,128]{3,2,1,0:T(8,128)(2,1)S(1)}, u32[]{:S(2)}, u32[]{:S(2)}) %collective-permute-start.6) | collective-permute-done | bytes 589856 | tf_op jit(solution)/shard_map/ppermute | solution.py:292
  78.6 0.0 copy-done.1
  78.6 2.5 %place.1 = f32[9,16,2048]{2,1,0:T(8,128)} custom-call(s32[8,8,16]{2,1,0:T(8,128)S(1)} %bitcast.9, bf16[16,9,16,128]{3,2,1,0:T(8,128)(2,1)S(1)} %all_to_all.11.own_ref, bf16[16,9,16,128]{3,2,1,0:T(8,128)(2,1)S(1)} %collective-permute-done.6.other_ref), custom_call_target="tpu_custom_call" | custom-call | tf_op jit(solution)/shard_map/place/pallas_call | solution.py:293
  (1 shorter events, 0.0 us)
Async XLA Ops:
  0.0 34.9 %collective-permute-start.3 = (bf16[8,2,32,128]{3,2,1,0:T(8,128)(2,1)}, bf16[8,2,32,128]{3,2,1,0:T(8,128)(2,1)S(1)}, u32[]{:S(2)}, u32[]{:S(2)}) collective-permute-start(bf16[8,2,32,128]{3,2,1,0:T(8,128)(2,1)} %bitcast.10), channel_id=1, source_target_pairs={{0,60},{4,0},{8,4},{12,8},{16,12},{20,16},{24,20},{28,24},{32,28},... | collective-permute-start | bytes 393224 | tf_op jit(solution)/shard_map/ppermute | solution.py:262
  6.4 28.5 %collective-permute-start.2 = (bf16[8,2,32,128]{3,2,1,0:T(8,128)(2,1)}, bf16[8,2,32,128]{3,2,1,0:T(8,128)(2,1)S(1)}, u32[]{:S(2)}, u32[]{:S(2)}) collective-permute-start(bf16[8,2,32,128]{3,2,1,0:T(8,128)(2,1)} %bitcast.11), channel_id=1, source_target_pairs={{0,4},{4,8},{8,12},{12,16},{16,20},{20,24},{24,28},{28,32},{32,36}... | collective-permute-start | bytes 393224 | tf_op jit(solution)/shard_map/ppermute | solution.py:261
  8.4 26.6 %collective-permute-start.1 = (bf16[8,2,32,128]{3,2,1,0:T(8,128)(2,1)}, bf16[8,2,32,128]{3,2,1,0:T(8,128)(2,1)S(1)}, u32[]{:S(2)}, u32[]{:S(2)}) collective-permute-start(bf16[8,2,32,128]{3,2,1,0:T(8,128)(2,1)} %bitcast.12), channel_id=1, source_target_pairs={{0,960},{64,0},{128,64},{192,128},{256,192},{320,256},{384,320},{4... | collective-permute-start | bytes 393224 | tf_op jit(solution)/shard_map/ppermute | solution.py:264
  20.0 15.0 %collective-permute-start = (bf16[8,2,32,128]{3,2,1,0:T(8,128)(2,1)}, bf16[8,2,32,128]{3,2,1,0:T(8,128)(2,1)S(1)}, u32[]{:S(2)}, u32[]{:S(2)}) collective-permute-start(bf16[8,2,32,128]{3,2,1,0:T(8,128)(2,1)} %bitcast.13), channel_id=1, source_target_pairs={{0,64},{64,128},{128,192},{192,256},{256,320},{320,384},{384,448},... | collective-permute-start | bytes 393224 | tf_op jit(solution)/shard_map/ppermute | solution.py:263
  20.0 0.9 %copy-start.2 = (bf16[1,1,8,2,32,128]{5,4,3,2,1,0:T(8,128)(2,1)S(1)}, bf16[1,1,8,2,32,128]{5,4,3,2,1,0:T(8,128)(2,1)}, u32[]{:S(2)}) copy-start(bf16[1,1,8,2,32,128]{5,4,3,2,1,0:T(8,128)(2,1)} %param.5) | copy-start | bytes 393220
  20.9 0.7 copy-start.3
  21.6 9.9 %copy-start = (bf16[1,1,8,2,9,64,128]{6,5,4,3,2,1,0:T(8,128)(2,1)S(1)}, bf16[1,1,8,2,9,64,128]{6,5,4,3,2,1,0:T(8,128)(2,1)}, u32[]{:S(2)}) copy-start(bf16[1,1,8,2,9,64,128]{6,5,4,3,2,1,0:T(8,128)(2,1)} %param.4) | copy-start | bytes 7077892
  22.9 6.6 %collective-permute-start.4 = (bf16[1,2,32,128]{3,2,1,0:T(8,128)(2,1)S(1)}, bf16[1,2,32,128]{3,2,1,0:T(8,128)(2,1)S(1)}, u32[]{:S(2)}, u32[]{:S(2)}) collective-permute-start(bf16[1,2,32,128]{3,2,1,0:T(8,128)(2,1)S(1)} %get-tuple-element.15), channel_id=1, source_target_pairs={{0,1},{1,2},{2,3},{3,0},{4,5},{5,6},{6,7},{7,4},{8,9},{9,10},{10,1... | collective-permute-start | bytes 49160 | tf_op jit(solution)/shard_map/ppermute | solution.py:259
  29.5 5.4 %collective-permute-start.5 = (bf16[1,2,32,128]{3,2,1,0:T(8,128)(2,1)S(1)}, bf16[1,2,32,128]{3,2,1,0:T(8,128)(2,1)S(1)}, u32[]{:S(2)}, u32[]{:S(2)}) collective-permute-start(bf16[1,2,32,128]{3,2,1,0:T(8,128)(2,1)S(1)} %get-tuple-element.16), channel_id=1, source_target_pairs={{0,3},{1,0},{2,1},{3,2},{4,7},{5,4},{6,5},{7,6},{8,11},{9,8},{10,9... | collective-permute-start | bytes 49160 | tf_op jit(solution)/shard_map/ppermute | solution.py:260
  34.9 43.7 %copy-start.1 = (s32[8,8,16,1]{2,3,1,0:T(1,128)S(1)}, s32[8,8,16,1]{2,3,1,0:T(1,128)}, u32[]{:S(2)}) copy-start(s32[8,8,16,1]{2,3,1,0:T(1,128)} %param.7) | copy-start | bytes 12292
  72.3 6.3 %collective-permute-start.6 = (bf16[16,9,16,128]{3,2,1,0:T(8,128)(2,1)S(1)}, bf16[16,9,16,128]{3,2,1,0:T(8,128)(2,1)S(1)}, u32[]{:S(2)}, u32[]{:S(2)}) collective-permute-start(bf16[16,9,16,128]{3,2,1,0:T(8,128)(2,1)S(1)} %all_to_all.11.own_ref), channel_id=1, source_target_pairs={{0,64},{64,0},{1,65},{65,1},{2,66},{66,2},{3,67},{67,3},{4,68},{68... | collective-permute-start | bytes 1769480 | tf_op jit(solution)/shard_map/ppermute | solution.py:292

commit v4 on v3

--- a/solution.py
+++ b/solution.py
@@ -53,26 +53,17 @@
     return role_ref[8], [role_ref[axis] for axis in range(4)], [role_ref[4 + axis] for axis in range(4)]
 
 
-def prepare_kernel(
-    off_ref, v_ref, role_ref, low_ref, high_ref, rows_ref, own_ref, first_ref, second_ref, vf_ref
-):
-    k_self = jnp.int32(36)
-    for place, (axis, sign) in enumerate([(a, g) for g in (-1, 1) for a in range(4)]):
-        index = jnp.int32(0)
-        for k in range(9):
-            index = index + jnp.where(off_ref[axis, k] == sign, k, 0).astype(jnp.int32)
-        role_ref[place] = index
-        k_self = k_self - index
-    role_ref[8] = k_self
-    low_ref[0] = v_ref[0]
-    high_ref[0] = v_ref[7]
+def prepare_kernel(v_ref, slab_ref, rows_ref, own_ref, vf_ref):
+    after = (lax.axis_index("gz") + 1) % 4
+    for step in range(1, 4):
+        slab_ref[(after + step) % 4] = v_ref[0]
+    slab_ref[after] = v_ref[7]
     signs = lane_signs()
     for z in range(8):
         for t in range(2):
             vf_ref[pl.ds((2 * z + t) * 32, 32), :] = v_ref[z, t].astype(F32)
             rows_ref[2 * z + t] = block_of(v_ref[z, t], signs)
     low = lane_index((16, 128)) < 64
-    low_own = lane_index((64, 128)) < 64
     for z in range(8):
         base = z * 64
         quarter = []
@@ -88,14 +79,29 @@
         half = jnp.concatenate([quarter[0][0], quarter[1][0], quarter[0][1], quarter[1][1]], 0)
         lanes = slice((z % 2) * 128, (z % 2) * 128 + 128)
         own_ref[z // 2, :, lanes] = half.astype(BF16)
-        first_ref[z // 2, :, lanes] = jnp.where(low_own, half, 0.0).astype(BF16)
-        second_ref[z // 2, :, lanes] = jnp.where(low_own, 0.0, half).astype(BF16)
 
 
 def inside_kernel(
-    off_ref, links_ref, rows_ref, own_ref, first_ref, second_ref, part_ref, acc_ref, hop_ref
+    off_ref,
+    links_ref,
+    rows_ref,
+    own_ref,
+    part_ref,
+    acc_ref,
+    role_ref,
+    hop_ref,
 ):
-    k_self, minus, plus = roles_of(off_ref)
+    k_self = jnp.int32(36)
+    found = []
+    for place, (axis, sign) in enumerate([(a, g) for g in (-1, 1) for a in range(4)]):
+        index = jnp.int32(0)
+        for k in range(9):
+            index = index + jnp.where(off_ref[axis, k] == sign, k, 0).astype(jnp.int32)
+        role_ref[place] = index
+        found.append(index)
+        k_self = k_self - index
+    role_ref[8] = k_self
+    minus, plus = found[:4], found[4:]
     for z in range(8):
         agg = z // 2
         for t in range(2):
@@ -123,11 +129,13 @@
             if 0 <= target <= 7:
                 row = 1024 + (2 * (target % 2) + t) * 64
                 hop_ref[target // 2, row : row + 64] = res[256:320]
+    first = jnp.where(lane_index((64, 256)) % 128 < 64, 1.0, 0.0).astype(BF16)
+    second = jnp.where(lane_index((64, 256)) % 128 < 64, 0.0, 1.0).astype(BF16)
     for agg in range(4):
         own = own_ref[agg]
         acc_ref[agg] = project(jnp.concatenate([own] * 3, 1), hop_ref[agg, 0:768])
-        part_ref[agg, 0] = fold(project(first_ref[agg], hop_ref[agg, 768:1024])).astype(BF16)
-        part_ref[agg, 1] = fold(project(second_ref[agg], hop_ref[agg, 768:1024])).astype(BF16)
+        part_ref[agg, 0] = fold(project(own * first, hop_ref[agg, 768:1024])).astype(BF16)
+        part_ref[agg, 1] = fold(project(own * second, hop_ref[agg, 768:1024])).astype(BF16)
         if agg > 0:
             part_ref[agg, 2] = fold(project(own[:, :128], hop_ref[agg, 1024:1152])).astype(BF16)
         if agg < 3:
@@ -143,8 +151,7 @@
     xh_ref,
     yl_ref,
     yh_ref,
-    zl_ref,
-    zh_ref,
+    z_ref,
     part_ref,
     acc_ref,
     own_ref,
@@ -155,6 +162,7 @@
     k_self, minus, plus = roles_of(role_ref)
     x_odd = lax.axis_index("xl")
     y_odd = lax.axis_index("yp")
+    block = lax.axis_index("gz")
     x_out = jnp.where(x_odd == 1, plus[0], minus[0])
     x_in = jnp.where(x_odd == 1, minus[0], plus[0])
     y_out = jnp.where(y_odd == 1, plus[1], minus[1])
@@ -170,8 +178,8 @@
         (yh_ref, plus[1], 256 + y_base),
     )
     for t in range(2):
-        rows_ref[64 + t] = block_of(zl_ref[0, t], signs)
-        rows_ref[66 + t] = block_of(zh_ref[0, t], signs)
+        rows_ref[64 + t] = block_of(z_ref[(block + 3) % 4, t], signs)
+        rows_ref[66 + t] = block_of(z_ref[(block + 1) % 4, t], signs)
     for z in range(8):
         for t in range(2):
             for role, (ref, _, _) in enumerate(sides):
@@ -205,14 +213,26 @@
             out_ref[agg, plus[2]] = fold(project(own[:, 128:], hop_ref[3, 1024:1152])).astype(BF16)
 
 
-def place_kernel(place_ref, own_ref, other_ref, out_ref, table_ref, wide_ref, buf_ref, sems):
+def gather_kernel(place_ref, own_ref, wide_ref, table_ref):
     line = lax.axis_index("xh")
     column = lax.axis_index("xl")
     block = lax.axis_index("gz")
-
     for entry in range(32):
-        target = place_ref[line, entry // 4, block * 4 + entry % 4]
-        table_ref[target] = jnp.int32(entry)
+        table_ref[place_ref[line, entry // 4, block * 4 + entry % 4]] = jnp.int32(entry)
+
+    def gather(slot, carry):
+        entry = table_ref[column * 16 + slot]
+        source = 2 * (entry // 4) + entry % 2
+        rows = pl.ds(pl.multiple_of(slot * 16, 16), 16)
+        for k in range(9):
+            wide_ref[k, rows, :] = own_ref[source, k].astype(F32)
+        return carry
+
+    lax.fori_loop(0, 16, gather, 0, unroll=4)
+
+
+def place_kernel(table_ref, other_ref, wide_ref, out_ref, work_ref, buf_ref, sems):
+    column = lax.axis_index("xl")
 
     def gather(slot, carry):
         entry = table_ref[column * 16 + slot]
@@ -220,15 +240,14 @@
         is_own = (entry % 4) // 2 == column
         rows = pl.ds(pl.multiple_of(slot * 16, 16), 16)
         for k in range(9):
-            picked = jnp.where(is_own, own_ref[source, k].astype(F32), other_ref[source, k].astype(F32))
-            wide_ref[k, rows, :] = picked
+            work_ref[k, rows, :] = jnp.where(is_own, wide_ref[k, rows, :], other_ref[source, k].astype(F32))
         return carry
 
     lax.fori_loop(0, 16, gather, 0, unroll=4)
     copies = []
     for k in range(9):
         for lane in range(16):
-            buf_ref[k, :, lane * 128 : (lane + 1) * 128] = wide_ref[k, pl.ds(lane, 16, stride=16), :]
+            buf_ref[k, :, lane * 128 : (lane + 1) * 128] = work_ref[k, pl.ds(lane, 16, stride=16), :]
         copies.append(pltpu.make_async_copy(buf_ref.at[k], out_ref.at[k], sems.at[k]))
         copies[k].start()
     for copy in copies:
@@ -241,69 +260,79 @@
     vmem = pl.BlockSpec(memory_space=pltpu.VMEM)
     smem = pl.BlockSpec(memory_space=pltpu.SMEM)
     anywhere = pl.BlockSpec(memory_space=pl.ANY)
-    role_table, slab_low, slab_high, rows, packed, packed_first, packed_second = pl.pallas_call(
+    slabs, rows, packed = pl.pallas_call(
         prepare_kernel,
-        out_shape=(jax.ShapeDtypeStruct((9,), jnp.int32),)
-        + (jax.ShapeDtypeStruct((1, 2, 32, 128), BF16),) * 2
+        out_shape=(jax.ShapeDtypeStruct((4, 2, 32, 128), BF16),)
         + (jax.ShapeDtypeStruct((16, 64, 128), BF16),)
-        + (jax.ShapeDtypeStruct((4, 64, 256), BF16),) * 3,
-        in_specs=[smem, vmem],
-        out_specs=(smem,) + (vmem,) * 6,
+        + (jax.ShapeDtypeStruct((4, 64, 256), BF16),),
+        in_specs=[vmem],
+        out_specs=(vmem,) * 3,
         scratch_shapes=[pltpu.VMEM((512, 128), F32)],
         compiler_params=pltpu.CompilerParams(vmem_limit_bytes=16 * 1024 * 1024),
         cost_estimate=pl.CostEstimate(
             flops=2_000_000_000, bytes_accessed=10_000_000, transcendentals=0
         ),
         name="prepare",
-    )(offsets.T, own)
-    z_low = lax.ppermute(slab_high, "gz", shift(4, 1))
-    z_high = lax.ppermute(slab_low, "gz", shift(4, -1))
+    )(own)
+    z_slabs = lax.all_to_all(slabs, "gz", 0, 0, tiled=True)
     y_low = lax.ppermute(own, GY, shift(16, 1))
     y_high = lax.ppermute(own, GY, shift(16, -1))
     x_low = lax.ppermute(own, GX, shift(16, 1))
     x_high = lax.ppermute(own, GX, shift(16, -1))
-    part, acc = pl.pallas_call(
+    part, acc, role_table = pl.pallas_call(
         inside_kernel,
         out_shape=(
             jax.ShapeDtypeStruct((4, 4, 16, 128), BF16),
             jax.ShapeDtypeStruct((4, 64, 64), F32),
+            jax.ShapeDtypeStruct((9,), jnp.int32),
         ),
-        in_specs=[smem] + [vmem] * 5,
-        out_specs=(vmem, vmem),
+        in_specs=[smem] + [vmem] * 3,
+        out_specs=(vmem, vmem, smem),
         scratch_shapes=[pltpu.VMEM((4, 1280, 64), BF16)],
         compiler_params=pltpu.CompilerParams(vmem_limit_bytes=16 * 1024 * 1024),
         cost_estimate=pl.CostEstimate(flops=150_000_000, bytes_accessed=3_000_000, transcendentals=0),
         name="inside",
-    )(role_table, links, rows, packed, packed_first, packed_second)
+    )(offsets.T, links, rows, packed)
     partial_value = pl.pallas_call(
         across_kernel,
         out_shape=jax.ShapeDtypeStruct((4, 9, 16, 128), BF16),
-        in_specs=[smem] + [vmem] * 10,
+        in_specs=[smem] + [vmem] * 9,
         out_specs=vmem,
         scratch_shapes=[pltpu.VMEM((68, 64, 128), BF16), pltpu.VMEM((4, 1152, 64), BF16)],
         compiler_params=pltpu.CompilerParams(vmem_limit_bytes=16 * 1024 * 1024),
         cost_estimate=pl.CostEstimate(flops=150_000_000, bytes_accessed=3_000_000, transcendentals=0),
         name="across",
-    )(role_table, links, x_low, x_high, y_low, y_high, z_low, z_high, part, acc, packed)
+    )(role_table, links, x_low, x_high, y_low, y_high, z_slabs, part, acc, packed)
     parts = lax.all_to_all(partial_value, ("xl", "yp"), 0, 0, tiled=True)
     chunk = jnp.sum(parts.astype(F32), axis=0).astype(BF16)
     spread = jnp.broadcast_to(chunk[None], (16, 9, 16, 128))
     mine = lax.all_to_all(spread, GY, 0, 0, tiled=True)
     other = lax.ppermute(mine, "xl", swap_inner(2))
+    wide, table = pl.pallas_call(
+        gather_kernel,
+        out_shape=(
+            jax.ShapeDtypeStruct((9, 256, 128), F32),
+            jax.ShapeDtypeStruct((32,), jnp.int32),
+        ),
+        in_specs=[smem, vmem],
+        out_specs=(vmem, smem),
+        compiler_params=pltpu.CompilerParams(vmem_limit_bytes=16 * 1024 * 1024),
+        cost_estimate=pl.CostEstimate(flops=1_000_000, bytes_accessed=3_000_000, transcendentals=0),
+        name="gather",
+    )(place.reshape(8, 8, 16), mine)
     placed = pl.pallas_call(
         place_kernel,
         out_shape=jax.ShapeDtypeStruct((9, 16, 2048), F32),
         in_specs=[smem, vmem, vmem],
         out_specs=anywhere,
         scratch_shapes=[
-            pltpu.SMEM((32,), jnp.int32),
             pltpu.VMEM((9, 256, 128), F32),
             pltpu.VMEM((9, 16, 2048), F32),
             pltpu.SemaphoreType.DMA((9,)),
         ],
         compiler_params=pltpu.CompilerParams(vmem_limit_bytes=32 * 1024 * 1024),
         name="place",
-    )(place.reshape(8, 8, 16), mine, other)
+    )(table, other, wide)
     return jnp.transpose(placed, (1, 0, 2))[None, None]
 
 

time: 81.5 us -> 80.8 us (level)
  waiting for transfers between devices: 8.33 us -> 5.26 us
  blocking collectives: 35.4 us -> 37.8 us
    ppermute x2 -> x0, waiting for transfers between devices: 6.71 us -> none  [the longest x1 4.66 us: local(): z_low = lax.ppermute(slab_high, 'gz', shift(4, 1))]
    all_to_all x0 -> x1, waiting for transfers between devices: none -> 5.25 us  [local(): z_slabs = lax.all_to_all(slabs, 'gz', 0, 0, tiled=True)]
    ppermute x2 -> x0, starting transfers between devices: 3.83 us -> none  [the longest x1 1.92 us: local(): z_low = lax.ppermute(slab_high, 'gz', shift(4, 1))]
    all_to_all x0 -> x1, starting transfers between devices: none -> 3.42 us  [local(): z_slabs = lax.all_to_all(slabs, 'gz', 0, 0, tiled=True)]
    all_to_all x1, blocking collectives: 12.9 us -> 15.3 us  [local(): parts = lax.all_to_all(partial_value, ('xl', 'yp'), 0, 0, tiled=True)]
    ppermute x1, waiting for transfers between devices: 1.61 us -> 0.01 us  [local(): other = lax.ppermute(mine, 'xl', swap_inner(2))]
    pallas_call x1 -> x2, Pallas kernels: 1.34 us -> 2.62 us  [the longest x1 1.9 us: local(): pl.pallas_call(gather_kernel, out_shape=(jax.ShapeDtypeStruct((9, 256, 12...]
  transfers between devices with their start and end apart: 7 -> 6, of which waited for: 3 -> 1; matrix products, arithmetic and copies ran while one was open for 0% -> 0% of each run, Pallas kernels for 3% -> 5%
where the time goes in v4:
time: 80.8 us; the launch traced here: 80.4 us
  blocking collectives  37.8 us (47%)
  starting transfers between devices  28.2 us (35%)
  Pallas kernels  7.93 us (10%)
  waiting for transfers between devices  5.26 us (7%)
  local copies, waits for them, and re-layouts  1.03 us (1%)
    all_to_all x1, blocking collectives, local(): mine = lax.all_to_all(spread, GY, 0, 0, tiled=True)  22.5 us
    all_to_all x1, blocking collectives, local(): parts = lax.all_to_all(partial_value, ('xl', 'yp'), 0, 0, tiled=True)  15.3 us
    ppermute x1, starting transfers between devices, local(): x_high = lax.ppermute(own, GX, shift(16, -1))  11.6 us
    ppermute x1, starting transfers between devices, local(): y_high = lax.ppermute(own, GY, shift(16, -1))  6.56 us
    all_to_all x1, waiting for transfers between devices, local(): z_slabs = lax.all_to_all(slabs, 'gz', 0, 0, tiled=True)  5.25 us
    ppermute x1, starting transfers between devices, local(): other = lax.ppermute(mine, 'xl', swap_inner(2))  4.69 us
    all_to_all x1, starting transfers between devices, local(): z_slabs = lax.all_to_all(slabs, 'gz', 0, 0, tiled=True)  3.42 us
    pallas_call x1, Pallas kernels, local(): pl.pallas_call(place_kernel, out_shape=jax.ShapeDtypeStruct((9, 16, 2048)...  1.93 us
  transfers between devices with their start and end apart: 6, of which 1 were waited for; matrix products, arithmetic and copies ran while one was open for 0% of the time, Pallas kernels for 5%

profile of v4, /device:TPU:1, one launch (start us, length us, event | category | flops | bytes accessed | tf_op | source)
XLA Modules:
  0.0 80.4 jit_solution(11221441184701281721)
XLA Ops:
  0.0 0.0 copy-start.2
  0.0 6.6 %collective-permute-start.3 = (bf16[8,2,32,128]{3,2,1,0:T(8,128)(2,1)}, bf16[8,2,32,128]{3,2,1,0:T(8,128)(2,1)S(1)}, u32[]{:S(2)}, u32[]{:S(2)}) collective-permute-start(bf16[8,2,32,128]{3,2,1,0:T(8,128)(2,1)} %bitcast.11), channel_id=1, source_target_pairs={{0,60},{4,0},{8,4},{12,8},{16,12},{20,16},{24,20},{28,24},{32,28},... | collective-permute-start | bytes 393224 | tf_op jit(solution)/shard_map/ppermute | solution.py:279
  6.6 1.9 %collective-permute-start.2 = (bf16[8,2,32,128]{3,2,1,0:T(8,128)(2,1)}, bf16[8,2,32,128]{3,2,1,0:T(8,128)(2,1)S(1)}, u32[]{:S(2)}, u32[]{:S(2)}) collective-permute-start(bf16[8,2,32,128]{3,2,1,0:T(8,128)(2,1)} %bitcast.12), channel_id=1, source_target_pairs={{0,4},{4,8},{8,12},{12,16},{16,20},{20,24},{24,28},{28,32},{32,36}... | collective-permute-start | bytes 393224 | tf_op jit(solution)/shard_map/ppermute | solution.py:278
  8.5 11.6 %collective-permute-start.1 = (bf16[8,2,32,128]{3,2,1,0:T(8,128)(2,1)}, bf16[8,2,32,128]{3,2,1,0:T(8,128)(2,1)S(1)}, u32[]{:S(2)}, u32[]{:S(2)}) collective-permute-start(bf16[8,2,32,128]{3,2,1,0:T(8,128)(2,1)} %bitcast.13), channel_id=1, source_target_pairs={{0,960},{64,0},{128,64},{192,128},{256,192},{320,256},{384,320},{4... | collective-permute-start | bytes 393224 | tf_op jit(solution)/shard_map/ppermute | solution.py:281
  20.1 0.0 collective-permute-start
  20.1 0.0 copy-start.3
  20.1 0.9 %copy-done.3 = bf16[1,1,8,2,32,128]{5,4,3,2,1,0:T(8,128)(2,1)S(1)} copy-done((bf16[1,1,8,2,32,128]{5,4,3,2,1,0:T(8,128)(2,1)S(1)}, bf16[1,1,8,2,32,128]{5,4,3,2,1,0:T(8,128)(2,1)}, u32[]{:S(2)}) %copy-start.3) | copy-done | bytes 131096
  21.0 0.0 copy-start
  21.1 0.7 prepare.1
  21.8 3.4 %all-to-all-start = ((bf16[4,2,32,128]{3,2,1,0:T(8,128)(2,1)}), bf16[4,2,32,128]{3,2,1,0:T(8,128)(2,1)S(1)}, u32[]{:S(2)}, u32[]{:S(2)}) async-start(bf16[4,2,32,128]{3,2,1,0:T(8,128)(2,1)} %get-tuple-element.16), calls=%async_computation | async-start | bytes 131072 | tf_op jit(solution)/shard_map/all_to_all | solution.py:277
  25.2 0.0 copy-done.2
  25.2 0.0 copy-done
  25.2 1.6 %inside.1 = (bf16[4,4,16,128]{3,2,1,0:T(8,128)(2,1)S(1)}, f32[4,64,64]{2,1,0:T(8,128)S(1)}, s32[9]{0:T(128)S(1)}) custom-call(s32[4,9]{1,0:T(4,128)S(1)} %bitcast.10, bf16[8,2,9,64,128]{4,3,2,1,0:T(8,128)(2,1)S(1)} %bitcast.7, bf16[16,64,128]{2,1,0:T(8,128)(2,1)S(1)} %get-tuple-element.13.rows_ref, bf16[4,64,256]{2,1,0:T(8,128)(2,1)S(1)} %get-tuple-element.14.own_ref), custom_call_target="tpu_custom_call" | custom-call | flops 150000000 | bytes 3000000 | tf_op jit(solution)/shard_map/inside/pallas_call | solution.py:282
  26.8 5.2 %all-to-all-done.z_ref = bf16[4,2,32,128]{3,2,1,0:T(8,128)(2,1)S(1)} async-done(((bf16[4,2,32,128]{3,2,1,0:T(8,128)(2,1)}), bf16[4,2,32,128]{3,2,1,0:T(8,128)(2,1)S(1)}, u32[]{:S(2)}, u32[]{:S(2)}) %all-to-all-start) | async-done | bytes 65568 | tf_op jit(solution)/shard_map/all_to_all | solution.py:277
  32.0 0.0 collective-permute-done.3.yh_ref
  32.0 0.0 collective-permute-done.2.yl_ref
  32.0 0.0 collective-permute-done.1.xh_ref
  32.1 0.0 collective-permute-done.xl_ref
  32.1 1.8 %across.1 = bf16[4,9,16,128]{3,2,1,0:T(8,128)(2,1)S(1)} custom-call(s32[9]{0:T(128)S(1)} %get-tuple-element.15.role_ref, bf16[8,2,9,64,128]{4,3,2,1,0:T(8,128)(2,1)S(1)} %bitcast.8, bf16[8,2,32,128]{3,2,1,0:T(8,128)(2,1)S(1)} %collective-permute-done.xl_ref, bf16[8,2,32,128]{3,2,1,0:T(8,128)(2,1)S(1)} %collective-permute-done.1.xh_ref, ...), custom_call_target="tpu_custom_call" | custom-call | flops 150000000 | bytes 3000000 | tf_op jit(solution)/shard_map/across/pallas_call | solution.py:296
  33.9 0.0 copy-start.1
  33.9 15.3 %all_to_all.15 = bf16[4,9,16,128]{3,2,1,0:T(8,128)(2,1)S(1)} all-to-all(bf16[4,9,16,128]{3,2,1,0:T(8,128)(2,1)S(1)} %across.1), channel_id=1, replica_groups=mesh['xh'=8,'xl'=2,'yl'=2,'yh'=4,'yp'=2,'gz'=4] {'xl','yp'}, dimensions={0} | all-to-all | bytes 294912 | tf_op jit(solution)/shard_map/all_to_all | solution.py:306
  49.2 0.1 broadcast_in_dim.4
  49.3 22.5 %all_to_all.16.own_ref = bf16[16,9,16,128]{3,2,1,0:T(8,128)(2,1)S(1)} all-to-all(bf16[16,9,16,128]{3,2,1,0:T(8,128)(2,1)S(1)} %broadcast_in_dim.4), channel_id=1, replica_groups=mesh['xh'=8,'xl'=2,'yl'=2,'yh'=4,'yp'=2,'gz'=4] {'yl','yh','yp'}, dimensions={0} | all-to-all | bytes 1179648 | tf_op jit(solution)/shard_map/all_to_all | solution.py:309
  71.8 4.7 %collective-permute-start.4 = (bf16[16,9,16,128]{3,2,1,0:T(8,128)(2,1)S(1)}, bf16[16,9,16,128]{3,2,1,0:T(8,128)(2,1)S(1)}, u32[]{:S(2)}, u32[]{:S(2)}) collective-permute-start(bf16[16,9,16,128]{3,2,1,0:T(8,128)(2,1)S(1)} %all_to_all.16.own_ref), channel_id=1, source_target_pairs={{0,64},{64,0},{1,65},{65,1},{2,66},{66,2},{3,67},{67,3},{4,68},{68... | collective-permute-start | bytes 1769480 | tf_op jit(solution)/shard_map/ppermute | solution.py:310
  76.5 0.0 copy-done.1
  76.5 1.9 %gather.1 = (f32[9,256,128]{2,1,0:T(8,128)S(1)}, s32[32]{0:T(128)S(1)}) custom-call(s32[8,8,16]{2,1,0:T(8,128)S(1)} %bitcast.9, bf16[16,9,16,128]{3,2,1,0:T(8,128)(2,1)S(1)} %all_to_all.16.own_ref), custom_call_target="tpu_custom_call" | custom-call | flops 1000000 | bytes 3000000 | tf_op jit(solution)/shard_map/gather/pallas_call | solution.py:311
  78.4 0.0 collective-permute-done.4.other_ref
  78.4 1.9 %place.1 = f32[9,16,2048]{2,1,0:T(8,128)} custom-call(s32[32]{0:T(128)S(1)} %get-tuple-element.19.table_ref, bf16[16,9,16,128]{3,2,1,0:T(8,128)(2,1)S(1)} %collective-permute-done.4.other_ref, f32[9,256,128]{2,1,0:T(8,128)S(1)} %get-tuple-element.20.wide_ref), custom_call_target="tpu_custom_call" | custom-call | tf_op jit(solution)/shard_map/place/pallas_call | solution.py:323
  (1 shorter events, 0.0 us)
Async XLA Ops:
  0.0 25.2 %copy-start.2 = (s32[9,4]{0,1:T(4,128)S(1)}, s32[9,4]{0,1:T(4,128)}, u32[]{:S(2)}) copy-start(s32[9,4]{0,1:T(4,128)} %param.6) | copy-start | bytes 436
  0.0 32.0 %collective-permute-start.3 = (bf16[8,2,32,128]{3,2,1,0:T(8,128)(2,1)}, bf16[8,2,32,128]{3,2,1,0:T(8,128)(2,1)S(1)}, u32[]{:S(2)}, u32[]{:S(2)}) collective-permute-start(bf16[8,2,32,128]{3,2,1,0:T(8,128)(2,1)} %bitcast.11), channel_id=1, source_target_pairs={{0,60},{4,0},{8,4},{12,8},{16,12},{20,16},{24,20},{28,24},{32,28},... | collective-permute-start | bytes 393224 | tf_op jit(solution)/shard_map/ppermute | solution.py:279
  6.6 25.5 %collective-permute-start.2 = (bf16[8,2,32,128]{3,2,1,0:T(8,128)(2,1)}, bf16[8,2,32,128]{3,2,1,0:T(8,128)(2,1)S(1)}, u32[]{:S(2)}, u32[]{:S(2)}) collective-permute-start(bf16[8,2,32,128]{3,2,1,0:T(8,128)(2,1)} %bitcast.12), channel_id=1, source_target_pairs={{0,4},{4,8},{8,12},{12,16},{16,20},{20,24},{24,28},{28,32},{32,36}... | collective-permute-start | bytes 393224 | tf_op jit(solution)/shard_map/ppermute | solution.py:278
  8.5 23.5 %collective-permute-start.1 = (bf16[8,2,32,128]{3,2,1,0:T(8,128)(2,1)}, bf16[8,2,32,128]{3,2,1,0:T(8,128)(2,1)S(1)}, u32[]{:S(2)}, u32[]{:S(2)}) collective-permute-start(bf16[8,2,32,128]{3,2,1,0:T(8,128)(2,1)} %bitcast.13), channel_id=1, source_target_pairs={{0,960},{64,0},{128,64},{192,128},{256,192},{320,256},{384,320},{4... | collective-permute-start | bytes 393224 | tf_op jit(solution)/shard_map/ppermute | solution.py:281
  20.1 12.0 %collective-permute-start = (bf16[8,2,32,128]{3,2,1,0:T(8,128)(2,1)}, bf16[8,2,32,128]{3,2,1,0:T(8,128)(2,1)S(1)}, u32[]{:S(2)}, u32[]{:S(2)}) collective-permute-start(bf16[8,2,32,128]{3,2,1,0:T(8,128)(2,1)} %bitcast.14), channel_id=1, source_target_pairs={{0,64},{64,128},{128,192},{192,256},{256,320},{320,384},{384,448},... | collective-permute-start | bytes 393224 | tf_op jit(solution)/shard_map/ppermute | solution.py:280
  20.1 0.9 %copy-start.3 = (bf16[1,1,8,2,32,128]{5,4,3,2,1,0:T(8,128)(2,1)S(1)}, bf16[1,1,8,2,32,128]{5,4,3,2,1,0:T(8,128)(2,1)}, u32[]{:S(2)}) copy-start(bf16[1,1,8,2,32,128]{5,4,3,2,1,0:T(8,128)(2,1)} %param.5) | copy-start | bytes 393220
  21.0 4.2 %copy-start = (bf16[1,1,8,2,9,64,128]{6,5,4,3,2,1,0:T(8,128)(2,1)S(1)}, bf16[1,1,8,2,9,64,128]{6,5,4,3,2,1,0:T(8,128)(2,1)}, u32[]{:S(2)}) copy-start(bf16[1,1,8,2,9,64,128]{6,5,4,3,2,1,0:T(8,128)(2,1)} %param.4) | copy-start | bytes 7077892
  21.8 10.3 %all-to-all-start = ((bf16[4,2,32,128]{3,2,1,0:T(8,128)(2,1)}), bf16[4,2,32,128]{3,2,1,0:T(8,128)(2,1)S(1)}, u32[]{:S(2)}, u32[]{:S(2)}) async-start(bf16[4,2,32,128]{3,2,1,0:T(8,128)(2,1)} %get-tuple-element.16), calls=%async_computation | async-start | bytes 131072 | tf_op jit(solution)/shard_map/all_to_all | solution.py:277
  33.9 42.6 %copy-start.1 = (s32[8,8,16,1]{2,3,1,0:T(1,128)S(1)}, s32[8,8,16,1]{2,3,1,0:T(1,128)}, u32[]{:S(2)}) copy-start(s32[8,8,16,1]{2,3,1,0:T(1,128)} %param.7) | copy-start | bytes 12292
  71.8 6.6 %collective-permute-start.4 = (bf16[16,9,16,128]{3,2,1,0:T(8,128)(2,1)S(1)}, bf16[16,9,16,128]{3,2,1,0:T(8,128)(2,1)S(1)}, u32[]{:S(2)}, u32[]{:S(2)}) collective-permute-start(bf16[16,9,16,128]{3,2,1,0:T(8,128)(2,1)S(1)} %all_to_all.16.own_ref), channel_id=1, source_target_pairs={{0,64},{64,0},{1,65},{65,1},{2,66},{66,2},{3,67},{67,3},{4,68},{68... | collective-permute-start | bytes 1769480 | tf_op jit(solution)/shard_map/ppermute | solution.py:310

commit v5 on v4

--- a/solution.py
+++ b/solution.py
@@ -53,11 +53,14 @@
     return role_ref[8], [role_ref[axis] for axis in range(4)], [role_ref[4 + axis] for axis in range(4)]
 
 
-def prepare_kernel(v_ref, slab_ref, rows_ref, own_ref, vf_ref):
+def slab_kernel(first_ref, last_ref, slab_ref):
     after = (lax.axis_index("gz") + 1) % 4
     for step in range(1, 4):
-        slab_ref[(after + step) % 4] = v_ref[0]
-    slab_ref[after] = v_ref[7]
+        slab_ref[(after + step) % 4] = first_ref[0]
+    slab_ref[after] = last_ref[0]
+
+
+def prepare_kernel(v_ref, rows_ref, own_ref, vf_ref):
     signs = lane_signs()
     for z in range(8):
         for t in range(2):
@@ -260,13 +263,14 @@
     vmem = pl.BlockSpec(memory_space=pltpu.VMEM)
     smem = pl.BlockSpec(memory_space=pltpu.SMEM)
     anywhere = pl.BlockSpec(memory_space=pl.ANY)
-    slabs, rows, packed = pl.pallas_call(
+    rows, packed = pl.pallas_call(
         prepare_kernel,
-        out_shape=(jax.ShapeDtypeStruct((4, 2, 32, 128), BF16),)
-        + (jax.ShapeDtypeStruct((16, 64, 128), BF16),)
-        + (jax.ShapeDtypeStruct((4, 64, 256), BF16),),
+        out_shape=(
+            jax.ShapeDtypeStruct((16, 64, 128), BF16),
+            jax.ShapeDtypeStruct((4, 64, 256), BF16),
+        ),
         in_specs=[vmem],
-        out_specs=(vmem,) * 3,
+        out_specs=(vmem,) * 2,
         scratch_shapes=[pltpu.VMEM((512, 128), F32)],
         compiler_params=pltpu.CompilerParams(vmem_limit_bytes=16 * 1024 * 1024),
         cost_estimate=pl.CostEstimate(
@@ -274,6 +278,17 @@
         ),
         name="prepare",
     )(own)
+    slabs = pl.pallas_call(
+        slab_kernel,
+        grid=(1,),
+        out_shape=jax.ShapeDtypeStruct((4, 2, 32, 128), BF16),
+        in_specs=[
+            pl.BlockSpec((1, 2, 32, 128), lambda i: (0, 0, 0, 0)),
+            pl.BlockSpec((1, 2, 32, 128), lambda i: (7, 0, 0, 0)),
+        ],
+        out_specs=pl.BlockSpec((4, 2, 32, 128), lambda i: (0, 0, 0, 0)),
+        name="slabs",
+    )(own, own)
     z_slabs = lax.all_to_all(slabs, "gz", 0, 0, tiled=True)
     y_low = lax.ppermute(own, GY, shift(16, 1))
     y_high = lax.ppermute(own, GY, shift(16, -1))

time: 80.8 us -> 80.4 us (level)
  waiting for transfers between devices: 5.26 us -> 2.71 us
  local copies, waits for them, and re-layouts: 1.03 us -> 2.5 us
  Pallas kernels: 7.93 us -> 8.75 us
    all_to_all x1, waiting for transfers between devices: 5.25 us -> 2.7 us  [local(): z_slabs = lax.all_to_all(slabs, 'gz', 0, 0, tiled=True)]
    unnamed x8, local copies, waits for them, and re-layouts: 0.95 us -> 2.42 us
    pallas_call x1 -> x2, Pallas kernels: 0.71 us -> 1.53 us  [the longest x1 1.39 us: local(): pl.pallas_call(slab_kernel, grid=(1,), out_shape=jax.ShapeDtypeStruct((4,...]
  transfers between devices with their start and end apart: 6 -> 6, of which waited for: 1 -> 1; matrix products, arithmetic and copies ran while one was open for 0% -> 0% of each run, Pallas kernels for 5% -> 6%
where the time goes in v5:
time: 80.4 us; the launch traced here: 79.8 us
  blocking collectives  37.8 us (47%)
  starting transfers between devices  27.9 us (35%)
  Pallas kernels  8.75 us (11%)
  waiting for transfers between devices  2.71 us (3%)
  local copies, waits for them, and re-layouts  2.5 us (3%)
    all_to_all x1, blocking collectives, local(): mine = lax.all_to_all(spread, GY, 0, 0, tiled=True)  22.5 us
    all_to_all x1, blocking collectives, local(): parts = lax.all_to_all(partial_value, ('xl', 'yp'), 0, 0, tiled=True)  15.3 us
    ppermute x1, starting transfers between devices, local(): x_high = lax.ppermute(own, GX, shift(16, -1))  11.6 us
    ppermute x1, starting transfers between devices, local(): y_high = lax.ppermute(own, GY, shift(16, -1))  6.43 us
    ppermute x1, starting transfers between devices, local(): other = lax.ppermute(mine, 'xl', swap_inner(2))  4.69 us
    all_to_all x1, starting transfers between devices, local(): z_slabs = lax.all_to_all(slabs, 'gz', 0, 0, tiled=True)  3.28 us
    all_to_all x1, waiting for transfers between devices, local(): z_slabs = lax.all_to_all(slabs, 'gz', 0, 0, tiled=True)  2.7 us
    unnamed x8, local copies, waits for them, and re-layouts  2.42 us
  transfers between devices with their start and end apart: 6, of which 1 were waited for; matrix products, arithmetic and copies ran while one was open for 0% of the time, Pallas kernels for 6%

profile of v5, /device:TPU:1, one launch (start us, length us, event | category | flops | bytes accessed | tf_op | source)
XLA Modules:
  0.0 79.8 jit_solution(2564717226419682461)
XLA Ops:
  0.0 6.4 %collective-permute-start.3 = (bf16[8,2,32,128]{3,2,1,0:T(8,128)(2,1)}, bf16[8,2,32,128]{3,2,1,0:T(8,128)(2,1)S(1)}, u32[]{:S(2)}, u32[]{:S(2)}) collective-permute-start(bf16[8,2,32,128]{3,2,1,0:T(8,128)(2,1)} %bitcast.9), channel_id=1, source_target_pairs={{0,60},{4,0},{8,4},{12,8},{16,12},{20,16},{24,20},{28,24},{32,28},... | collective-permute-start | bytes 393224 | tf_op jit(solution)/shard_map/ppermute | solution.py:294
  6.4 1.9 %collective-permute-start.2 = (bf16[8,2,32,128]{3,2,1,0:T(8,128)(2,1)}, bf16[8,2,32,128]{3,2,1,0:T(8,128)(2,1)S(1)}, u32[]{:S(2)}, u32[]{:S(2)}) collective-permute-start(bf16[8,2,32,128]{3,2,1,0:T(8,128)(2,1)} %bitcast.10), channel_id=1, source_target_pairs={{0,4},{4,8},{8,12},{12,16},{16,20},{20,24},{24,28},{28,32},{32,36}... | collective-permute-start | bytes 393224 | tf_op jit(solution)/shard_map/ppermute | solution.py:293
  8.4 11.6 %collective-permute-start.1 = (bf16[8,2,32,128]{3,2,1,0:T(8,128)(2,1)}, bf16[8,2,32,128]{3,2,1,0:T(8,128)(2,1)S(1)}, u32[]{:S(2)}, u32[]{:S(2)}) collective-permute-start(bf16[8,2,32,128]{3,2,1,0:T(8,128)(2,1)} %bitcast.11), channel_id=1, source_target_pairs={{0,960},{64,0},{128,64},{192,128},{256,192},{320,256},{384,320},{4... | collective-permute-start | bytes 393224 | tf_op jit(solution)/shard_map/ppermute | solution.py:296
  20.0 0.0 collective-permute-start
  20.0 1.4 %slabs.1 = bf16[4,2,32,128]{3,2,1,0:T(8,128)(2,1)} custom-call(bf16[8,2,32,128]{3,2,1,0:T(8,128)(2,1)} %bitcast.13, bf16[8,2,32,128]{3,2,1,0:T(8,128)(2,1)} %bitcast.14), custom_call_target="tpu_custom_call" | custom-call | tf_op jit(solution)/shard_map/slabs/pallas_call | solution.py:281
  21.4 3.3 %all-to-all-start = ((bf16[4,2,32,128]{3,2,1,0:T(8,128)(2,1)}), bf16[4,2,32,128]{3,2,1,0:T(8,128)(2,1)S(1)}, u32[]{:S(2)}, u32[]{:S(2)}) async-start(bf16[4,2,32,128]{3,2,1,0:T(8,128)(2,1)} %slabs.1), calls=%async_computation | async-start | bytes 131072 | tf_op jit(solution)/shard_map/all_to_all | solution.py:292
  24.7 0.0 copy-start.1
  24.7 0.9 %copy-done.1 = bf16[1,1,8,2,32,128]{5,4,3,2,1,0:T(8,128)(2,1)S(1)} copy-done((bf16[1,1,8,2,32,128]{5,4,3,2,1,0:T(8,128)(2,1)S(1)}, bf16[1,1,8,2,32,128]{5,4,3,2,1,0:T(8,128)(2,1)}, u32[]{:S(2)}) %copy-start.1) | copy-done | bytes 131096
  25.6 0.0 copy-start
  25.6 0.0 copy-start.3
  25.6 0.1 prepare.1
  25.7 1.5 %copy-done = bf16[1,1,8,2,9,64,128]{6,5,4,3,2,1,0:T(8,128)(2,1)S(1)} copy-done((bf16[1,1,8,2,9,64,128]{6,5,4,3,2,1,0:T(8,128)(2,1)S(1)}, bf16[1,1,8,2,9,64,128]{6,5,4,3,2,1,0:T(8,128)(2,1)}, u32[]{:S(2)}) %copy-start) | copy-done | bytes 2359320
  27.2 0.0 copy-done.3
  27.2 1.6 %inside.1 = (bf16[4,4,16,128]{3,2,1,0:T(8,128)(2,1)S(1)}, f32[4,64,64]{2,1,0:T(8,128)S(1)}, s32[9]{0:T(128)S(1)}) custom-call(s32[4,9]{1,0:T(4,128)S(1)} %bitcast.17, bf16[8,2,9,64,128]{4,3,2,1,0:T(8,128)(2,1)S(1)} %bitcast.7, bf16[16,64,128]{2,1,0:T(8,128)(2,1)S(1)} %get-tuple-element.12.rows_ref, bf16[4,64,256]{2,1,0:T(8,128)(2,1)S(1)} %get-tuple-element.13.own_ref), custom_call_target="tpu_custom_call" | custom-call | flops 150000000 | bytes 3000000 | tf_op jit(solution)/shard_map/inside/pallas_call | solution.py:297
  28.8 2.7 %all-to-all-done.z_ref = bf16[4,2,32,128]{3,2,1,0:T(8,128)(2,1)S(1)} async-done(((bf16[4,2,32,128]{3,2,1,0:T(8,128)(2,1)}), bf16[4,2,32,128]{3,2,1,0:T(8,128)(2,1)S(1)}, u32[]{:S(2)}, u32[]{:S(2)}) %all-to-all-start) | async-done | bytes 65568 | tf_op jit(solution)/shard_map/all_to_all | solution.py:292
  31.5 0.0 collective-permute-done.3.yh_ref
  31.5 0.0 collective-permute-done.2.yl_ref
  31.5 0.0 collective-permute-done.1.xh_ref
  31.5 0.0 collective-permute-done.xl_ref
  31.5 1.8 %across.1 = bf16[4,9,16,128]{3,2,1,0:T(8,128)(2,1)S(1)} custom-call(s32[9]{0:T(128)S(1)} %get-tuple-element.14.role_ref, bf16[8,2,9,64,128]{4,3,2,1,0:T(8,128)(2,1)S(1)} %bitcast.8, bf16[8,2,32,128]{3,2,1,0:T(8,128)(2,1)S(1)} %collective-permute-done.xl_ref, bf16[8,2,32,128]{3,2,1,0:T(8,128)(2,1)S(1)} %collective-permute-done.1.xh_ref, ...), custom_call_target="tpu_custom_call" | custom-call | flops 150000000 | bytes 3000000 | tf_op jit(solution)/shard_map/across/pallas_call | solution.py:311
  33.4 0.0 copy-start.2
  33.4 15.3 %all_to_all.15 = bf16[4,9,16,128]{3,2,1,0:T(8,128)(2,1)S(1)} all-to-all(bf16[4,9,16,128]{3,2,1,0:T(8,128)(2,1)S(1)} %across.1), channel_id=1, replica_groups=mesh['xh'=8,'xl'=2,'yl'=2,'yh'=4,'yp'=2,'gz'=4] {'xl','yp'}, dimensions={0} | all-to-all | bytes 294912 | tf_op jit(solution)/shard_map/all_to_all | solution.py:321
  48.7 0.1 broadcast_in_dim.4
  48.8 22.5 %all_to_all.16.own_ref = bf16[16,9,16,128]{3,2,1,0:T(8,128)(2,1)S(1)} all-to-all(bf16[16,9,16,128]{3,2,1,0:T(8,128)(2,1)S(1)} %broadcast_in_dim.4), channel_id=1, replica_groups=mesh['xh'=8,'xl'=2,'yl'=2,'yh'=4,'yp'=2,'gz'=4] {'yl','yh','yp'}, dimensions={0} | all-to-all | bytes 1179648 | tf_op jit(solution)/shard_map/all_to_all | solution.py:324
  71.3 4.7 %collective-permute-start.4 = (bf16[16,9,16,128]{3,2,1,0:T(8,128)(2,1)S(1)}, bf16[16,9,16,128]{3,2,1,0:T(8,128)(2,1)S(1)}, u32[]{:S(2)}, u32[]{:S(2)}) collective-permute-start(bf16[16,9,16,128]{3,2,1,0:T(8,128)(2,1)S(1)} %all_to_all.16.own_ref), channel_id=1, source_target_pairs={{0,64},{64,0},{1,65},{65,1},{2,66},{66,2},{3,67},{67,3},{4,68},{68... | collective-permute-start | bytes 1769480 | tf_op jit(solution)/shard_map/ppermute | solution.py:325
  76.0 0.0 copy-done.2
  76.0 1.9 %gather.1 = (f32[9,256,128]{2,1,0:T(8,128)S(1)}, s32[32]{0:T(128)S(1)}) custom-call(s32[8,8,16]{2,1,0:T(8,128)S(1)} %bitcast.16, bf16[16,9,16,128]{3,2,1,0:T(8,128)(2,1)S(1)} %all_to_all.16.own_ref), custom_call_target="tpu_custom_call" | custom-call | flops 1000000 | bytes 3000000 | tf_op jit(solution)/shard_map/gather/pallas_call | solution.py:326
  77.9 0.0 collective-permute-done.4.other_ref
  77.9 1.9 %place.1 = f32[9,16,2048]{2,1,0:T(8,128)} custom-call(s32[32]{0:T(128)S(1)} %get-tuple-element.17.table_ref, bf16[16,9,16,128]{3,2,1,0:T(8,128)(2,1)S(1)} %collective-permute-done.4.other_ref, f32[9,256,128]{2,1,0:T(8,128)S(1)} %get-tuple-element.18.wide_ref), custom_call_target="tpu_custom_call" | custom-call | tf_op jit(solution)/shard_map/place/pallas_call | solution.py:338
  (1 shorter events, 0.0 us)
Async XLA Ops:
  0.0 31.5 %collective-permute-start.3 = (bf16[8,2,32,128]{3,2,1,0:T(8,128)(2,1)}, bf16[8,2,32,128]{3,2,1,0:T(8,128)(2,1)S(1)}, u32[]{:S(2)}, u32[]{:S(2)}) collective-permute-start(bf16[8,2,32,128]{3,2,1,0:T(8,128)(2,1)} %bitcast.9), channel_id=1, source_target_pairs={{0,60},{4,0},{8,4},{12,8},{16,12},{20,16},{24,20},{28,24},{32,28},... | collective-permute-start | bytes 393224 | tf_op jit(solution)/shard_map/ppermute | solution.py:294
  6.4 25.1 %collective-permute-start.2 = (bf16[8,2,32,128]{3,2,1,0:T(8,128)(2,1)}, bf16[8,2,32,128]{3,2,1,0:T(8,128)(2,1)S(1)}, u32[]{:S(2)}, u32[]{:S(2)}) collective-permute-start(bf16[8,2,32,128]{3,2,1,0:T(8,128)(2,1)} %bitcast.10), channel_id=1, source_target_pairs={{0,4},{4,8},{8,12},{12,16},{16,20},{20,24},{24,28},{28,32},{32,36}... | collective-permute-start | bytes 393224 | tf_op jit(solution)/shard_map/ppermute | solution.py:293
  8.4 23.2 %collective-permute-start.1 = (bf16[8,2,32,128]{3,2,1,0:T(8,128)(2,1)}, bf16[8,2,32,128]{3,2,1,0:T(8,128)(2,1)S(1)}, u32[]{:S(2)}, u32[]{:S(2)}) collective-permute-start(bf16[8,2,32,128]{3,2,1,0:T(8,128)(2,1)} %bitcast.11), channel_id=1, source_target_pairs={{0,960},{64,0},{128,64},{192,128},{256,192},{320,256},{384,320},{4... | collective-permute-start | bytes 393224 | tf_op jit(solution)/shard_map/ppermute | solution.py:296
  20.0 11.6 %collective-permute-start = (bf16[8,2,32,128]{3,2,1,0:T(8,128)(2,1)}, bf16[8,2,32,128]{3,2,1,0:T(8,128)(2,1)S(1)}, u32[]{:S(2)}, u32[]{:S(2)}) collective-permute-start(bf16[8,2,32,128]{3,2,1,0:T(8,128)(2,1)} %bitcast.12), channel_id=1, source_target_pairs={{0,64},{64,128},{128,192},{192,256},{256,320},{320,384},{384,448},... | collective-permute-start | bytes 393224 | tf_op jit(solution)/shard_map/ppermute | solution.py:295
  21.4 10.1 %all-to-all-start = ((bf16[4,2,32,128]{3,2,1,0:T(8,128)(2,1)}), bf16[4,2,32,128]{3,2,1,0:T(8,128)(2,1)S(1)}, u32[]{:S(2)}, u32[]{:S(2)}) async-start(bf16[4,2,32,128]{3,2,1,0:T(8,128)(2,1)} %slabs.1), calls=%async_computation | async-start | bytes 131072 | tf_op jit(solution)/shard_map/all_to_all | solution.py:292
  24.7 0.9 %copy-start.1 = (bf16[1,1,8,2,32,128]{5,4,3,2,1,0:T(8,128)(2,1)S(1)}, bf16[1,1,8,2,32,128]{5,4,3,2,1,0:T(8,128)(2,1)}, u32[]{:S(2)}) copy-start(bf16[1,1,8,2,32,128]{5,4,3,2,1,0:T(8,128)(2,1)} %param.5) | copy-start | bytes 393220
  25.6 1.7 %copy-start = (bf16[1,1,8,2,9,64,128]{6,5,4,3,2,1,0:T(8,128)(2,1)S(1)}, bf16[1,1,8,2,9,64,128]{6,5,4,3,2,1,0:T(8,128)(2,1)}, u32[]{:S(2)}) copy-start(bf16[1,1,8,2,9,64,128]{6,5,4,3,2,1,0:T(8,128)(2,1)} %param.4) | copy-start | bytes 7077892
  25.6 1.7 %copy-start.3 = (s32[9,4]{0,1:T(4,128)S(1)}, s32[9,4]{0,1:T(4,128)}, u32[]{:S(2)}) copy-start(s32[9,4]{0,1:T(4,128)} %param.6) | copy-start | bytes 436
  33.4 42.6 %copy-start.2 = (s32[8,8,16,1]{2,3,1,0:T(1,128)S(1)}, s32[8,8,16,1]{2,3,1,0:T(1,128)}, u32[]{:S(2)}) copy-start(s32[8,8,16,1]{2,3,1,0:T(1,128)} %param.7) | copy-start | bytes 12292
  71.3 6.6 %collective-permute-start.4 = (bf16[16,9,16,128]{3,2,1,0:T(8,128)(2,1)S(1)}, bf16[16,9,16,128]{3,2,1,0:T(8,128)(2,1)S(1)}, u32[]{:S(2)}, u32[]{:S(2)}) collective-permute-start(bf16[16,9,16,128]{3,2,1,0:T(8,128)(2,1)S(1)} %all_to_all.16.own_ref), channel_id=1, source_target_pairs={{0,64},{64,0},{1,65},{65,1},{2,66},{66,2},{3,67},{67,3},{4,68},{68... | collective-permute-start | bytes 1769480 | tf_op jit(solution)/shard_map/ppermute | solution.py:325

commit v6 on v5

--- a/solution.py
+++ b/solution.py
@@ -13,6 +13,14 @@
 
 def swap_inner(count):
     return [(i, i ^ 1) for i in range(count)]
+
+
+def swap_outer(count):
+    pairs = []
+    for i in range(count):
+        step = 1 if i % 2 else -1
+        pairs.append((i, (i + step) % count))
+    return pairs
 
 
 def shift(count, step):
@@ -152,8 +160,8 @@
     links_ref,
     xl_ref,
     xh_ref,
-    yl_ref,
-    yh_ref,
+    ya_ref,
+    yb_ref,
     z_ref,
     part_ref,
     acc_ref,
@@ -171,14 +179,13 @@
     y_out = jnp.where(y_odd == 1, plus[1], minus[1])
     y_in = jnp.where(y_odd == 1, minus[1], plus[1])
     x_base = pl.multiple_of(512 * x_odd, 256)
-    y_base = pl.multiple_of(512 * y_odd, 256)
     zero = jnp.zeros((16, 128), BF16)
     signs = lane_signs()
     sides = (
         (xl_ref, minus[0], 512 - x_base),
         (xh_ref, plus[0], x_base),
-        (yl_ref, minus[1], 768 - y_base),
-        (yh_ref, plus[1], 256 + y_base),
+        (ya_ref, y_in, 256),
+        (yb_ref, y_out, 768),
     )
     for t in range(2):
         rows_ref[64 + t] = block_of(z_ref[(block + 3) % 4, t], signs)
@@ -193,7 +200,8 @@
     for z in range(8):
         for t in range(2):
             for role, (_, k, base) in enumerate(sides):
-                row = pl.multiple_of(base + (2 * (z % 2) + t) * 64, 64)
+                row = base + (2 * (z % 2) + t) * 64
+                row = row if isinstance(row, int) else pl.multiple_of(row, 64)
                 res = hop(links_ref[z, t, k], rows_ref[role * 16 + 2 * z + t])
                 hop_ref[z // 2, pl.ds(row, 64)] = res
     for agg in range(4):
@@ -273,9 +281,7 @@
         out_specs=(vmem,) * 2,
         scratch_shapes=[pltpu.VMEM((512, 128), F32)],
         compiler_params=pltpu.CompilerParams(vmem_limit_bytes=16 * 1024 * 1024),
-        cost_estimate=pl.CostEstimate(
-            flops=2_000_000_000, bytes_accessed=10_000_000, transcendentals=0
-        ),
+        cost_estimate=pl.CostEstimate(flops=1_000_000, bytes_accessed=500_000, transcendentals=0),
         name="prepare",
     )(own)
     slabs = pl.pallas_call(
@@ -287,11 +293,14 @@
             pl.BlockSpec((1, 2, 32, 128), lambda i: (7, 0, 0, 0)),
         ],
         out_specs=pl.BlockSpec((4, 2, 32, 128), lambda i: (0, 0, 0, 0)),
+        cost_estimate=pl.CostEstimate(
+            flops=2_000_000_000, bytes_accessed=10_000_000, transcendentals=0
+        ),
         name="slabs",
     )(own, own)
     z_slabs = lax.all_to_all(slabs, "gz", 0, 0, tiled=True)
-    y_low = lax.ppermute(own, GY, shift(16, 1))
-    y_high = lax.ppermute(own, GY, shift(16, -1))
+    y_outer = lax.ppermute(own, GY, swap_outer(16))
+    y_inner = lax.ppermute(own, "yp", swap_inner(2))
     x_low = lax.ppermute(own, GX, shift(16, 1))
     x_high = lax.ppermute(own, GX, shift(16, -1))
     part, acc, role_table = pl.pallas_call(
@@ -317,7 +326,7 @@
         compiler_params=pltpu.CompilerParams(vmem_limit_bytes=16 * 1024 * 1024),
         cost_estimate=pl.CostEstimate(flops=150_000_000, bytes_accessed=3_000_000, transcendentals=0),
         name="across",
-    )(role_table, links, x_low, x_high, y_low, y_high, z_slabs, part, acc, packed)
+    )(role_table, links, x_low, x_high, y_inner, y_outer, z_slabs, part, acc, packed)
     parts = lax.all_to_all(partial_value, ("xl", "yp"), 0, 0, tiled=True)
     chunk = jnp.sum(parts.astype(F32), axis=0).astype(BF16)
     spread = jnp.broadcast_to(chunk[None], (16, 9, 16, 128))

time: 80.4 us -> 79.8 us (level)
  local copies, waits for them, and re-layouts: 2.5 us -> 0.1 us
  waiting for transfers between devices: 2.71 us -> 5.1 us
  starting transfers between devices: 27.9 us -> 26.1 us
  blocking collectives: 37.8 us -> 39 us
    all_to_all x1, blocking collectives: 15.3 us -> 17.7 us  [local(): parts = lax.all_to_all(partial_value, ('xl', 'yp'), 0, 0, tiled=True)]
    unnamed x8, local copies, waits for them, and re-layouts: 2.42 us -> 0.02 us
    all_to_all x1, waiting for transfers between devices: 2.7 us -> 5.09 us  [local(): z_slabs = lax.all_to_all(slabs, 'gz', 0, 0, tiled=True)]
    ppermute x1, starting transfers between devices: 11.6 us -> 9.6 us  [local(): x_high = lax.ppermute(own, GX, shift(16, -1))]
    all_to_all x1, blocking collectives: 22.5 us -> 21.3 us  [local(): mine = lax.all_to_all(spread, GY, 0, 0, tiled=True)]
where the time goes in v6:
time: 79.8 us; the launch traced here: 79.3 us
  blocking collectives  39 us (49%)
  starting transfers between devices  26.1 us (33%)
  Pallas kernels  8.85 us (11%)
  waiting for transfers between devices  5.1 us (6%)
    all_to_all x1, blocking collectives, local(): mine = lax.all_to_all(spread, GY, 0, 0, tiled=True)  21.3 us
    all_to_all x1, blocking collectives, local(): parts = lax.all_to_all(partial_value, ('xl', 'yp'), 0, 0, tiled=True)  17.7 us
    ppermute x1, starting transfers between devices, local(): x_high = lax.ppermute(own, GX, shift(16, -1))  9.6 us
    ppermute x1, starting transfers between devices, local(): y_outer = lax.ppermute(own, GY, swap_outer(16))  6.56 us
    all_to_all x1, waiting for transfers between devices, local(): z_slabs = lax.all_to_all(slabs, 'gz', 0, 0, tiled=True)  5.09 us
    ppermute x1, starting transfers between devices, local(): other = lax.ppermute(mine, 'xl', swap_inner(2))  4.69 us
    all_to_all x1, starting transfers between devices, local(): z_slabs = lax.all_to_all(slabs, 'gz', 0, 0, tiled=True)  3.28 us
    pallas_call x1, Pallas kernels, local(): pl.pallas_call(place_kernel, out_shape=jax.ShapeDtypeStruct((9, 16, 2048)...  1.93 us
  transfers between devices with their start and end apart: 6, of which 1 were waited for; matrix products, arithmetic and copies ran while one was open for 0% of the time, Pallas kernels for 6%

profile of v6, /device:TPU:1, one launch (start us, length us, event | category | flops | bytes accessed | tf_op | source)
XLA Modules:
  0.0 79.3 jit_solution(9873259462981341589)
XLA Ops:
  0.0 0.0 copy-start.1
  0.0 0.0 copy-start.3
  0.0 6.6 %collective-permute-start.3 = (bf16[8,2,32,128]{3,2,1,0:T(8,128)(2,1)}, bf16[8,2,32,128]{3,2,1,0:T(8,128)(2,1)S(1)}, u32[]{:S(2)}, u32[]{:S(2)}) collective-permute-start(bf16[8,2,32,128]{3,2,1,0:T(8,128)(2,1)} %bitcast.9), channel_id=1, source_target_pairs={{0,60},{4,8},{8,4},{12,16},{16,12},{20,24},{24,20},{28,32},{32,28}... | collective-permute-start | bytes 393224 | tf_op jit(solution)/shard_map/ppermute | solution.py:302
  6.6 1.9 %collective-permute-start.2 = (bf16[8,2,32,128]{3,2,1,0:T(8,128)(2,1)}, bf16[8,2,32,128]{3,2,1,0:T(8,128)(2,1)S(1)}, u32[]{:S(2)}, u32[]{:S(2)}) collective-permute-start(bf16[8,2,32,128]{3,2,1,0:T(8,128)(2,1)} %bitcast.10), channel_id=1, source_target_pairs={{0,4},{4,0},{1,5},{5,1},{2,6},{6,2},{3,7},{7,3},{8,12},{12,8},{9,1... | collective-permute-start | bytes 393224 | tf_op jit(solution)/shard_map/ppermute | solution.py:303
  8.5 9.6 %collective-permute-start.1 = (bf16[8,2,32,128]{3,2,1,0:T(8,128)(2,1)}, bf16[8,2,32,128]{3,2,1,0:T(8,128)(2,1)S(1)}, u32[]{:S(2)}, u32[]{:S(2)}) collective-permute-start(bf16[8,2,32,128]{3,2,1,0:T(8,128)(2,1)} %bitcast.11), channel_id=1, source_target_pairs={{0,960},{64,0},{128,64},{192,128},{256,192},{320,256},{384,320},{4... | collective-permute-start | bytes 393224 | tf_op jit(solution)/shard_map/ppermute | solution.py:305
  18.1 0.0 collective-permute-start
  18.1 0.0 copy-start
  18.1 1.5 %slabs.1 = bf16[4,2,32,128]{3,2,1,0:T(8,128)(2,1)} custom-call(bf16[8,2,32,128]{3,2,1,0:T(8,128)(2,1)} %bitcast.13, bf16[8,2,32,128]{3,2,1,0:T(8,128)(2,1)} %bitcast.14), custom_call_target="tpu_custom_call" | custom-call | flops 2000000000 | bytes 10000000 | tf_op jit(solution)/shard_map/slabs/pallas_call | solution.py:287
  19.6 3.3 %all-to-all-start = ((bf16[4,2,32,128]{3,2,1,0:T(8,128)(2,1)}), bf16[4,2,32,128]{3,2,1,0:T(8,128)(2,1)S(1)}, u32[]{:S(2)}, u32[]{:S(2)}) async-start(bf16[4,2,32,128]{3,2,1,0:T(8,128)(2,1)} %slabs.1), calls=%async_computation | async-start | bytes 131072 | tf_op jit(solution)/shard_map/all_to_all | solution.py:301
  22.9 0.0 copy-done.1
  22.9 0.1 prepare.1
  23.1 0.0 copy-done.3
  23.1 0.0 copy-done
  23.1 1.6 %inside.1 = (bf16[4,4,16,128]{3,2,1,0:T(8,128)(2,1)S(1)}, f32[4,64,64]{2,1,0:T(8,128)S(1)}, s32[9]{0:T(128)S(1)}) custom-call(s32[4,9]{1,0:T(4,128)S(1)} %bitcast.17, bf16[8,2,9,64,128]{4,3,2,1,0:T(8,128)(2,1)S(1)} %bitcast.7, bf16[16,64,128]{2,1,0:T(8,128)(2,1)S(1)} %get-tuple-element.12.rows_ref, bf16[4,64,256]{2,1,0:T(8,128)(2,1)S(1)} %get-tuple-element.13.own_ref), custom_call_target="tpu_custom_call" | custom-call | flops 150000000 | bytes 3000000 | tf_op jit(solution)/shard_map/inside/pallas_call | solution.py:306
  24.7 5.1 %all-to-all-done.z_ref = bf16[4,2,32,128]{3,2,1,0:T(8,128)(2,1)S(1)} async-done(((bf16[4,2,32,128]{3,2,1,0:T(8,128)(2,1)}), bf16[4,2,32,128]{3,2,1,0:T(8,128)(2,1)S(1)}, u32[]{:S(2)}, u32[]{:S(2)}) %all-to-all-start) | async-done | bytes 65568 | tf_op jit(solution)/shard_map/all_to_all | solution.py:301
  29.8 0.0 collective-permute-done.3.yb_ref
  29.8 0.0 collective-permute-done.2.ya_ref
  29.8 0.0 collective-permute-done.1.xh_ref
  29.8 0.0 collective-permute-done.xl_ref
  29.8 1.8 %across.1 = bf16[4,9,16,128]{3,2,1,0:T(8,128)(2,1)S(1)} custom-call(s32[9]{0:T(128)S(1)} %get-tuple-element.14.role_ref, bf16[8,2,9,64,128]{4,3,2,1,0:T(8,128)(2,1)S(1)} %bitcast.8, bf16[8,2,32,128]{3,2,1,0:T(8,128)(2,1)S(1)} %collective-permute-done.xl_ref, bf16[8,2,32,128]{3,2,1,0:T(8,128)(2,1)S(1)} %collective-permute-done.1.xh_ref, ...), custom_call_target="tpu_custom_call" | custom-call | flops 150000000 | bytes 3000000 | tf_op jit(solution)/shard_map/across/pallas_call | solution.py:320
  31.6 0.0 copy-start.2
  31.6 17.7 %all_to_all.15 = bf16[4,9,16,128]{3,2,1,0:T(8,128)(2,1)S(1)} all-to-all(bf16[4,9,16,128]{3,2,1,0:T(8,128)(2,1)S(1)} %across.1), channel_id=1, replica_groups=mesh['xh'=8,'xl'=2,'yl'=2,'yh'=4,'yp'=2,'gz'=4] {'xl','yp'}, dimensions={0} | all-to-all | bytes 294912 | tf_op jit(solution)/shard_map/all_to_all | solution.py:330
  49.4 0.1 broadcast_in_dim.4
  49.4 21.3 %all_to_all.16.own_ref = bf16[16,9,16,128]{3,2,1,0:T(8,128)(2,1)S(1)} all-to-all(bf16[16,9,16,128]{3,2,1,0:T(8,128)(2,1)S(1)} %broadcast_in_dim.4), channel_id=1, replica_groups=mesh['xh'=8,'xl'=2,'yl'=2,'yh'=4,'yp'=2,'gz'=4] {'yl','yh','yp'}, dimensions={0} | all-to-all | bytes 1179648 | tf_op jit(solution)/shard_map/all_to_all | solution.py:333
  70.8 4.7 %collective-permute-start.4 = (bf16[16,9,16,128]{3,2,1,0:T(8,128)(2,1)S(1)}, bf16[16,9,16,128]{3,2,1,0:T(8,128)(2,1)S(1)}, u32[]{:S(2)}, u32[]{:S(2)}) collective-permute-start(bf16[16,9,16,128]{3,2,1,0:T(8,128)(2,1)S(1)} %all_to_all.16.own_ref), channel_id=1, source_target_pairs={{0,64},{64,0},{1,65},{65,1},{2,66},{66,2},{3,67},{67,3},{4,68},{68... | collective-permute-start | bytes 1769480 | tf_op jit(solution)/shard_map/ppermute | solution.py:334
  75.4 0.0 copy-done.2
  75.5 1.9 %gather.1 = (f32[9,256,128]{2,1,0:T(8,128)S(1)}, s32[32]{0:T(128)S(1)}) custom-call(s32[8,8,16]{2,1,0:T(8,128)S(1)} %bitcast.16, bf16[16,9,16,128]{3,2,1,0:T(8,128)(2,1)S(1)} %all_to_all.16.own_ref), custom_call_target="tpu_custom_call" | custom-call | flops 1000000 | bytes 3000000 | tf_op jit(solution)/shard_map/gather/pallas_call | solution.py:335
  77.4 0.0 collective-permute-done.4.other_ref
  77.4 1.9 %place.1 = f32[9,16,2048]{2,1,0:T(8,128)} custom-call(s32[32]{0:T(128)S(1)} %get-tuple-element.17.table_ref, bf16[16,9,16,128]{3,2,1,0:T(8,128)(2,1)S(1)} %collective-permute-done.4.other_ref, f32[9,256,128]{2,1,0:T(8,128)S(1)} %get-tuple-element.18.wide_ref), custom_call_target="tpu_custom_call" | custom-call | tf_op jit(solution)/shard_map/place/pallas_call | solution.py:347
  (1 shorter events, 0.0 us)
Async XLA Ops:
  0.0 22.9 %copy-start.1 = (bf16[1,1,8,2,32,128]{5,4,3,2,1,0:T(8,128)(2,1)S(1)}, bf16[1,1,8,2,32,128]{5,4,3,2,1,0:T(8,128)(2,1)}, u32[]{:S(2)}) copy-start(bf16[1,1,8,2,32,128]{5,4,3,2,1,0:T(8,128)(2,1)} %param.5) | copy-start | bytes 393220
  0.0 23.1 %copy-start.3 = (s32[9,4]{0,1:T(4,128)S(1)}, s32[9,4]{0,1:T(4,128)}, u32[]{:S(2)}) copy-start(s32[9,4]{0,1:T(4,128)} %param.6) | copy-start | bytes 436
  0.0 29.8 %collective-permute-start.3 = (bf16[8,2,32,128]{3,2,1,0:T(8,128)(2,1)}, bf16[8,2,32,128]{3,2,1,0:T(8,128)(2,1)S(1)}, u32[]{:S(2)}, u32[]{:S(2)}) collective-permute-start(bf16[8,2,32,128]{3,2,1,0:T(8,128)(2,1)} %bitcast.9), channel_id=1, source_target_pairs={{0,60},{4,8},{8,4},{12,16},{16,12},{20,24},{24,20},{28,32},{32,28}... | collective-permute-start | bytes 393224 | tf_op jit(solution)/shard_map/ppermute | solution.py:302
  6.6 23.2 %collective-permute-start.2 = (bf16[8,2,32,128]{3,2,1,0:T(8,128)(2,1)}, bf16[8,2,32,128]{3,2,1,0:T(8,128)(2,1)S(1)}, u32[]{:S(2)}, u32[]{:S(2)}) collective-permute-start(bf16[8,2,32,128]{3,2,1,0:T(8,128)(2,1)} %bitcast.10), channel_id=1, source_target_pairs={{0,4},{4,0},{1,5},{5,1},{2,6},{6,2},{3,7},{7,3},{8,12},{12,8},{9,1... | collective-permute-start | bytes 393224 | tf_op jit(solution)/shard_map/ppermute | solution.py:303
  8.5 21.3 %collective-permute-start.1 = (bf16[8,2,32,128]{3,2,1,0:T(8,128)(2,1)}, bf16[8,2,32,128]{3,2,1,0:T(8,128)(2,1)S(1)}, u32[]{:S(2)}, u32[]{:S(2)}) collective-permute-start(bf16[8,2,32,128]{3,2,1,0:T(8,128)(2,1)} %bitcast.11), channel_id=1, source_target_pairs={{0,960},{64,0},{128,64},{192,128},{256,192},{320,256},{384,320},{4... | collective-permute-start | bytes 393224 | tf_op jit(solution)/shard_map/ppermute | solution.py:305
  18.1 11.7 %collective-permute-start = (bf16[8,2,32,128]{3,2,1,0:T(8,128)(2,1)}, bf16[8,2,32,128]{3,2,1,0:T(8,128)(2,1)S(1)}, u32[]{:S(2)}, u32[]{:S(2)}) collective-permute-start(bf16[8,2,32,128]{3,2,1,0:T(8,128)(2,1)} %bitcast.12), channel_id=1, source_target_pairs={{0,64},{64,128},{128,192},{192,256},{256,320},{320,384},{384,448},... | collective-permute-start | bytes 393224 | tf_op jit(solution)/shard_map/ppermute | solution.py:304
  18.1 5.0 %copy-start = (bf16[1,1,8,2,9,64,128]{6,5,4,3,2,1,0:T(8,128)(2,1)S(1)}, bf16[1,1,8,2,9,64,128]{6,5,4,3,2,1,0:T(8,128)(2,1)}, u32[]{:S(2)}) copy-start(bf16[1,1,8,2,9,64,128]{6,5,4,3,2,1,0:T(8,128)(2,1)} %param.4) | copy-start | bytes 7077892
  19.6 10.1 %all-to-all-start = ((bf16[4,2,32,128]{3,2,1,0:T(8,128)(2,1)}), bf16[4,2,32,128]{3,2,1,0:T(8,128)(2,1)S(1)}, u32[]{:S(2)}, u32[]{:S(2)}) async-start(bf16[4,2,32,128]{3,2,1,0:T(8,128)(2,1)} %slabs.1), calls=%async_computation | async-start | bytes 131072 | tf_op jit(solution)/shard_map/all_to_all | solution.py:301
  31.6 43.9 %copy-start.2 = (s32[8,8,16,1]{2,3,1,0:T(1,128)S(1)}, s32[8,8,16,1]{2,3,1,0:T(1,128)}, u32[]{:S(2)}) copy-start(s32[8,8,16,1]{2,3,1,0:T(1,128)} %param.7) | copy-start | bytes 12292
  70.8 6.6 %collective-permute-start.4 = (bf16[16,9,16,128]{3,2,1,0:T(8,128)(2,1)S(1)}, bf16[16,9,16,128]{3,2,1,0:T(8,128)(2,1)S(1)}, u32[]{:S(2)}, u32[]{:S(2)}) collective-permute-start(bf16[16,9,16,128]{3,2,1,0:T(8,128)(2,1)S(1)} %all_to_all.16.own_ref), channel_id=1, source_target_pairs={{0,64},{64,0},{1,65},{65,1},{2,66},{66,2},{3,67},{67,3},{4,68},{68... | collective-permute-start | bytes 1769480 | tf_op jit(solution)/shard_map/ppermute | solution.py:334
